TPU v7x, 32 devices: a whole 2x2x4 slice. The times are simulated.
32 devices in a mesh: seq: 4 (over y, x), fsdp: 8 (over z, core).
Axes of the slice: x: 2, y: 2, z: 4, core: 2. Of those that a mesh axis runs over, the one named last changes fastest.
Arguments:
- block_input: bfloat16 [8, 2048, 1024], P('fsdp', 'seq'), may hold values from -6 to 6
- norm_gain_a: float32 [1024], P('fsdp'), may hold values from 0.1 to 1.9
- weight_qkv: float32 [1024, 3072], P('fsdp'), may hold values from -0.1875 to 0.1875
- weight_out: float32 [1024, 1024], P('fsdp'), may hold values from -3 to 3
- norm_gain_b: float32 [1024], P('fsdp'), may hold values from 0.1 to 1.9
- weight_gate_up: float32 [1024, 8192], P('fsdp'), may hold values from -0.1875 to 0.1875
- weight_down: float32 [1024, 4096], P('fsdp'), may hold values from -0.09375 to 0.09375
- cotangent: bfloat16 [8, 2048, 1024], P('fsdp', 'seq'), may hold values from -6 to 6
- permutation: int32 [8, 2048], P('fsdp'), may hold values from 0 to 2047, each once within a row
- lengths: int32 [8, 3], P('fsdp'), may hold values from 256 to 1024, as said below
- offsets: int32 [8, 3], P('fsdp'), may hold values from 0 to 1792, as said below
Outputs:
- block_output: bfloat16 [8, 2048, 1024], P('fsdp', 'seq')
- grad_input: bfloat16 [8, 2048, 1024], P('fsdp', 'seq')
- grad_gain_a: float32 [1024], P('fsdp')
- grad_qkv: float32 [1024, 3072], P('fsdp')
- grad_out: float32 [1024, 1024], P('fsdp')
- grad_gain_b: float32 [1024], P('fsdp')
- grad_gate_up: float32 [1024, 8192], P('fsdp')
- grad_down: float32 [1024, 4096], P('fsdp')
Inputs may be any that keep to these rules, and one draw needn't show every extreme that they name: A group's 3 lengths sum to 2048, and its longest is exactly 1024. offsets[g, k] is the sum of lengths[g, i] over i < k, so that a group's sequences tile its positions.
All inputs are finite; a program needn't handle non-finite values.
Results may differ from a plain program's by a relative error of at most 0.02.
Values may be sent and summed in bfloat16 or wider, within the bound.
A program may use at most 256 MiB of HBM per device.

v0:
```python
import jax
import jax.numpy as jnp
from jax import lax
from jax.experimental import pallas as pl
from jax.experimental.pallas import tpu as pltpu
from jax.sharding import PartitionSpec as P

HEAD_DIM = 64
BLK = 256
LOG2E = 1.4426950408889634

NT = (((1,), (1,)), ((), ()))
NN = (((1,), (0,)), ((), ()))


def dot(a, b, dims=NN):
    return lax.dot_general(a, b, dims, preferred_element_type=jnp.float32)


def first_block(offs_ref, row0):
    best = jnp.int32(0)
    for k in range(offs_ref.shape[0]):
        off = offs_ref[k]
        best = jnp.where(off <= row0, jnp.maximum(best, off), best)
    return best // BLK


def sort_rows(perm_row_ref, src_ref, dst_ref):
    group_len = src_ref.shape[0]

    def step(i, carry):
        rows = pl.ds(pl.multiple_of(i * BLK, BLK), BLK)
        pos = lax.broadcasted_iota(jnp.int32, (BLK, group_len), 0) + i * BLK
        pick = (perm_row_ref[...] == pos).astype(jnp.float32).astype(jnp.bfloat16)
        dst_ref[rows, :] = dot(pick, src_ref[...]).astype(dst_ref.dtype)
        return carry

    lax.fori_loop(0, group_len // BLK, step, 0)


def deal_rows(perm_col_ref, src_ref, dst_ref, out_ref, sems):
    group_len = src_ref.shape[0]

    def copy_out(i):
        rows = pl.ds(pl.multiple_of(i * BLK, BLK), BLK)
        return pltpu.make_async_copy(dst_ref.at[rows, :], out_ref.at[rows, :], sems.at[i])

    def step(i, carry):
        rows = pl.ds(pl.multiple_of(i * BLK, BLK), BLK)
        pos = lax.broadcasted_iota(jnp.int32, (BLK, group_len), 1)
        pick = (perm_col_ref[rows, :] == pos).astype(jnp.float32).astype(jnp.bfloat16)
        dst_ref[rows, :] = dot(pick, src_ref[...]).astype(dst_ref.dtype)
        copy_out(i).start()
        return carry

    def wait(i, carry):
        copy_out(i).wait()
        return carry

    lax.fori_loop(0, group_len // BLK, step, 0)
    lax.fori_loop(0, group_len // BLK, wait, 0)


def allowed_block(start_ref, cols, qb, kb):
    key_pos = lax.broadcasted_iota(jnp.int32, (BLK, BLK), 0) + kb * BLK
    query_pos = lax.broadcasted_iota(jnp.int32, (BLK, BLK), 1) + qb * BLK
    return (key_pos <= query_pos) & (key_pos >= start_ref[:, cols])


def forward_kernel(offs_ref, x_ref, slab_ref, perm_row_ref, perm_col_ref, start_ref,
                   sorted_out, dealt_out, wide_out, lse_ref, normed_out, gains_ref,
                   sorted_ref, dealt_ref, wide_ref, normed_ref, qkv_ref, vt_ref, low_ref, local_sem, deal_sem):
    group_len, model = x_ref.shape
    width = qkv_ref.shape[1] // 3
    heads = width // HEAD_DIM
    scale = HEAD_DIM ** -0.5 * LOG2E

    def gain(i, carry):
        part = pl.ds(pl.multiple_of(i * 128, 128), 128)
        gains_ref[:, part] = slab_ref[part, 3 * width:].astype(jnp.float32).T[:8]
        return carry

    lax.fori_loop(0, model // 128, gain, 0)

    def project(i, carry):
        rows = pl.ds(pl.multiple_of(i * BLK, BLK), BLK)
        for r in range(0, BLK, 64):
            part = pl.ds(pl.multiple_of(i * BLK + r, 64), 64)
            x = x_ref[part, :].astype(jnp.float32)
            normed_ref[part, :] = (x * rms_scale(x) * gains_ref[0:1, :]).astype(jnp.bfloat16)
        qkv_ref[rows, :] = dot(normed_ref[rows, :], slab_ref[:, :3 * width]).astype(jnp.bfloat16)
        return carry

    lax.fori_loop(0, group_len // BLK, project, 0)
    outs = [pltpu.make_async_copy(normed_ref, normed_out, local_sem.at[0])]
    outs[0].start()
    sort_rows(perm_row_ref, qkv_ref, sorted_ref)
    outs.append(pltpu.make_async_copy(sorted_ref, sorted_out, local_sem.at[1]))
    outs[1].start()

    def flip(i, carry):
        rows = pl.ds(pl.multiple_of(i * BLK, BLK), BLK)
        vt_ref[:, rows] = sorted_ref[rows, 2 * width:].T
        return carry

    lax.fori_loop(0, group_len // BLK, flip, 0)

    def query_step(qb, carry):
        qrow = pl.multiple_of(qb * BLK, BLK)
        cols = pl.ds(qrow, BLK)

        def key_step(kb, state):
            krow = pl.multiple_of(kb * BLK, BLK)
            krows = pl.ds(krow, BLK)
            allowed = allowed_block(start_ref, cols, qb, kb)
            fresh = []
            for h in range(heads):
                top, total, acc = state[3 * h: 3 * h + 3]
                hq = slice(h * HEAD_DIM, (h + 1) * HEAD_DIM)
                hk = slice(width + h * HEAD_DIM, width + (h + 1) * HEAD_DIM)
                s = dot(sorted_ref[krows, hk], sorted_ref[cols, hq], NT) * scale
                s = jnp.where(allowed, s, -1e30)
                new_top = jnp.maximum(top, jnp.max(s, axis=0, keepdims=True))
                shrink = jnp.exp2(top - new_top)
                p = jnp.exp2(s - new_top)
                total = total * shrink + jnp.sum(p, axis=0, keepdims=True)
                acc = acc * shrink + dot(vt_ref[hq, krows], p.astype(jnp.bfloat16))
                fresh += [new_top, total, acc]
            return tuple(fresh)

        init = []
        for h in range(heads):
            init += [jnp.full((1, BLK), -1e30, jnp.float32), jnp.zeros((1, BLK), jnp.float32),
                     jnp.zeros((HEAD_DIM, BLK), jnp.float32)]
        state = lax.fori_loop(first_block(offs_ref, qrow), qb + 1, key_step, tuple(init))
        parts = []
        for h in range(heads):
            top, total, acc = state[3 * h: 3 * h + 3]
            out = acc / total
            wide_ref[h * HEAD_DIM:(h + 1) * HEAD_DIM, cols] = out
            lse_ref[h:h + 1, cols] = top + jnp.log2(total)
            parts.append(out)
        low_ref[cols, :] = jnp.concatenate(parts, axis=0).T.astype(jnp.bfloat16)
        return carry

    lax.fori_loop(0, group_len // BLK, query_step, 0)
    outs.append(pltpu.make_async_copy(wide_ref, wide_out, local_sem.at[2]))
    outs[2].start()
    deal_rows(perm_col_ref, low_ref, dealt_ref, dealt_out, deal_sem)
    for copy in outs:
        copy.wait()


def backward_kernel(offs_ref, grad_ref, sorted_in, perm_row_ref, perm_col_ref, start_ref, wide_in, lse_ref,
                    dealt_out, sorted_ref, wide_ref, dealt_ref, do_ref, kt_ref, delta_ref, dk_ref, dv_ref, low_ref,
                    local_sem, deal_sem):
    copies = [pltpu.make_async_copy(sorted_in, sorted_ref, local_sem.at[0]),
              pltpu.make_async_copy(wide_in, wide_ref, local_sem.at[1])]
    for copy in copies:
        copy.start()
    group_len = sorted_ref.shape[0]
    width = sorted_ref.shape[1] // 3
    heads = width // HEAD_DIM
    unit = HEAD_DIM ** -0.5
    scale = unit * LOG2E
    sort_rows(perm_row_ref, grad_ref, do_ref)
    dk_ref[...] = jnp.zeros_like(dk_ref)
    dv_ref[...] = jnp.zeros_like(dv_ref)
    for copy in copies:
        copy.wait()

    def flip(i, carry):
        rows = pl.ds(pl.multiple_of(i * BLK, BLK), BLK)
        kt_ref[:, rows] = sorted_ref[rows, width: 2 * width].T
        product = do_ref[rows, :].astype(jnp.float32).T * wide_ref[:, rows]
        for h in range(heads):
            delta_ref[h:h + 1, rows] = jnp.sum(product[h * HEAD_DIM:(h + 1) * HEAD_DIM], axis=0, keepdims=True)
        return carry

    lax.fori_loop(0, group_len // BLK, flip, 0)

    def query_step(qb, carry):
        qrow = pl.multiple_of(qb * BLK, BLK)
        cols = pl.ds(qrow, BLK)

        def key_step(kb, state):
            krow = pl.multiple_of(kb * BLK, BLK)
            krows = pl.ds(krow, BLK)
            allowed = allowed_block(start_ref, cols, qb, kb)
            fresh = []
            for h in range(heads):
                hq = slice(h * HEAD_DIM, (h + 1) * HEAD_DIM)
                hk = slice(width + h * HEAD_DIM, width + (h + 1) * HEAD_DIM)
                hv = slice(2 * width + h * HEAD_DIM, 2 * width + (h + 1) * HEAD_DIM)
                q = sorted_ref[cols, hq]
                do = do_ref[cols, hq]
                s = dot(sorted_ref[krows, hk], q, NT) * scale
                s = jnp.where(allowed, s, -1e30)
                p = jnp.exp2(s - lse_ref[h:h + 1, cols])
                dp = dot(sorted_ref[krows, hv], do, NT)
                ds = (p * (dp - delta_ref[h:h + 1, cols])).astype(jnp.bfloat16)
                dv_ref[krows, hq] += dot(p.astype(jnp.bfloat16), do)
                dk_ref[krows, hq] += dot(ds, q)
                fresh.append(state[h] + dot(kt_ref[hq, krows], ds))
            return tuple(fresh)

        state = lax.fori_loop(first_block(offs_ref, qrow), qb + 1, key_step,
                              tuple(jnp.zeros((HEAD_DIM, BLK), jnp.float32) for _ in range(heads)))
        low_ref[cols, :width] = (jnp.concatenate(state, axis=0) * unit).T.astype(jnp.bfloat16)
        return carry

    lax.fori_loop(0, group_len // BLK, query_step, 0)
    low_ref[:, width:2 * width] = (dk_ref[...] * unit).astype(jnp.bfloat16)
    low_ref[:, 2 * width:] = dv_ref[...].astype(jnp.bfloat16)
    deal_rows(perm_col_ref, low_ref, dealt_ref, dealt_out, deal_sem)


def hbm():
    return pl.BlockSpec(memory_space=pltpu.HBM)


def vmem():
    return pl.BlockSpec(memory_space=pltpu.VMEM)


def attention_forward(offs, rows, slab, perm, start):
    group_len, model = rows.shape
    columns = slab.shape[1] - 128
    width = columns // 3
    shape = jax.ShapeDtypeStruct
    return pl.pallas_call(
        forward_kernel,
        name="attention_forward",
        out_shape=(
            shape((group_len, columns), jnp.bfloat16),
            shape((group_len, width), jnp.bfloat16),
            shape((width, group_len), jnp.float32),
            shape((8, group_len), jnp.float32),
            shape((group_len, model), jnp.bfloat16),
            shape((8, model), jnp.float32),
        ),
        in_specs=[pl.BlockSpec(memory_space=pltpu.SMEM)] + [vmem()] * 5,
        out_specs=(hbm(), hbm(), hbm(), vmem(), hbm(), vmem()),
        scratch_shapes=[
            pltpu.VMEM((group_len, columns), jnp.bfloat16),
            pltpu.VMEM((group_len, width), jnp.bfloat16),
            pltpu.VMEM((width, group_len), jnp.float32),
            pltpu.VMEM((group_len, model), jnp.bfloat16),
            pltpu.VMEM((group_len, columns), jnp.bfloat16),
            pltpu.VMEM((width, group_len), jnp.bfloat16),
            pltpu.VMEM((group_len, width), jnp.bfloat16),
            pltpu.SemaphoreType.DMA((3,)),
            pltpu.SemaphoreType.DMA((group_len // BLK,)),
        ],
        compiler_params=pltpu.CompilerParams(vmem_limit_bytes=48 << 20),
        cost_estimate=pl.CostEstimate(flops=24_000_000_000, bytes_accessed=16 << 20, transcendentals=0),
    )(offs, rows, slab, perm.reshape(1, group_len), perm.reshape(group_len, 1), start.reshape(1, group_len))


def attention_backward(offs, grad, ordered, perm, start, wide, lse):
    group_len, columns = ordered.shape
    width = columns // 3
    return pl.pallas_call(
        backward_kernel,
        name="attention_backward",
        out_shape=jax.ShapeDtypeStruct((group_len, columns), jnp.bfloat16),
        in_specs=[pl.BlockSpec(memory_space=pltpu.SMEM), vmem(), hbm(), vmem(), vmem(), vmem(), hbm(), vmem()],
        out_specs=hbm(),
        scratch_shapes=[
            pltpu.VMEM((group_len, columns), jnp.bfloat16),
            pltpu.VMEM((width, group_len), jnp.float32),
            pltpu.VMEM((group_len, columns), jnp.bfloat16),
            pltpu.VMEM((group_len, width), jnp.bfloat16),
            pltpu.VMEM((width, group_len), jnp.bfloat16),
            pltpu.VMEM((8, group_len), jnp.float32),
            pltpu.VMEM((group_len, width), jnp.float32),
            pltpu.VMEM((group_len, width), jnp.float32),
            pltpu.VMEM((group_len, columns), jnp.bfloat16),
            pltpu.SemaphoreType.DMA((2,)),
            pltpu.SemaphoreType.DMA((group_len // BLK,)),
        ],
        compiler_params=pltpu.CompilerParams(vmem_limit_bytes=48 << 20),
        cost_estimate=pl.CostEstimate(flops=40_000_000_000, bytes_accessed=16 << 20, transcendentals=0),
    )(offs, grad, ordered, perm.reshape(1, group_len), perm.reshape(group_len, 1), start.reshape(1, group_len), wide, lse)


epsilon = 1e-05


def rms_scale(values):
    return lax.rsqrt(jnp.mean(values * values, axis=-1, keepdims=True) + epsilon)


MESH = pl.DeviceIdType.MESH
TN = (((0,), (0,)), ((), ()))
TILE = 256


def seq_peers():
    mine = lax.axis_index("seq")
    return mine, (mine + 1 - 2 * lax.rem(mine, 2), lax.rem(mine + 2, 4), 3 - mine)


def greet(peers, others=()):
    barrier = pltpu.get_barrier_semaphore()
    for peer in others:
        pl.semaphore_signal(barrier, inc=1, device_id={"fsdp": peer}, device_id_type=MESH)
    for peer in peers:
        pl.semaphore_signal(barrier, inc=1, device_id={"seq": peer}, device_id_type=MESH)
    return lambda: pl.semaphore_wait(barrier, len(peers) + len(others))


def span(index, size):
    return pl.ds(pl.multiple_of(index * size, size), size)


def sender(send_sem, recv_sem):
    def send(index, src, dst, axis, peer):
        return pltpu.make_async_remote_copy(
            src_ref=src, dst_ref=dst, send_sem=send_sem.at[index], recv_sem=recv_sem.at[index],
            device_id={axis: peer}, device_id_type=MESH)
    return send


def shard_peers(count):
    mine = lax.axis_index("fsdp")
    sibling = mine + 1 - 2 * lax.rem(mine, 2)
    return mine, sibling, [lax.rem(mine + 2 * k, count) for k in range(1, count // 2)]


def starter(local_sem):
    def local(index, src, dst):
        copy = pltpu.make_async_copy(src, dst, local_sem.at[index])
        copy.start()
        return copy
    return local


def pair_sum(send, base, place, sibling, others, source, twin, total, take, shard):
    count = 2 * (len(others) + 1)
    twins = [send(base + k, source(span(lax.rem(sibling + 2 * k, count), shard)), twin.at[k], "fsdp", sibling)
             for k in range(count // 2)]
    direct = [send(base + count // 2 + k, total.at[k], take.at[k], "fsdp", others[k - 1]) for k in range(1, count // 2)]

    def start():
        for copy in twins:
            copy.start()

    def pass_on():
        for k in range(1, count // 2) :
            twins[k].wait_recv()
            total[k] = (source(span(lax.rem(place + 2 * k, count), shard))[...].astype(jnp.float32)
                        + twin[k].astype(jnp.float32)).astype(jnp.bfloat16)
            direct[k - 1].start()

    def finish(out_ref):
        twins[0].wait_recv()
        value = source(span(place, shard))[...].astype(jnp.float32) + twin[0].astype(jnp.float32)
        for k in range(1, count // 2):
            direct[k - 1].wait()
            value += take[k].astype(jnp.float32)
        out_ref[...] = value.astype(jnp.bfloat16)
        for copy in twins:
            copy.wait_send()

    return start, pass_on, finish


def spread(send, base, own, slots, peers):
    px, py, _ = peers
    half = own.shape[0] // 2
    top, bottom = pl.ds(0, half), pl.ds(half, half)
    x_slot, y_slot, far_slot = slots
    x_top = send(base, own.at[top], x_slot.at[top], "seq", px)
    y_bottom = send(base + 1, own.at[bottom], y_slot.at[bottom], "seq", py)
    x_bottom = send(base + 2, own.at[bottom], x_slot.at[bottom], "seq", px)
    y_top = send(base + 3, own.at[top], y_slot.at[top], "seq", py)
    x_relay = send(base + 4, x_slot.at[top], far_slot.at[top], "seq", py)
    y_relay = send(base + 5, y_slot.at[bottom], far_slot.at[bottom], "seq", px)
    for copy in (x_top, y_bottom, x_bottom, y_top):
        copy.start()

    def forward():
        x_top.wait_recv()
        x_relay.start()
        y_bottom.wait_recv()
        y_relay.start()

    def finish():
        for copy in (x_top, y_bottom, x_bottom, y_top, x_relay, y_relay):
            copy.wait_send()

    return forward, (x_bottom.wait_recv, y_top.wait_recv, lambda: (x_relay.wait_recv(), y_relay.wait_recv())), finish


def collect(send, base, give, transit, take, peers, cut):
    px, py, _ = peers
    half = give.shape[1] // 2
    size = half // cut
    halves = (pl.ds(0, half), pl.ds(half, half))
    pieces = [[pl.ds(h * half + c * size, size) for c in range(cut)] for h in range(2)]
    first, second = (px, py), (py, px)
    far = [[send(base + h * cut + c, give.at[2, pieces[h][c]], transit.at[h, pl.ds(c * size, size)], "seq", first[h])
            for c in range(cut)] for h in range(2)]
    plain = [send(base + 2 * cut + h, give.at[h, halves[h]], take.at[h, halves[h]], "seq", first[h]) for h in range(2)]
    summed = [[send(base + 2 * cut + 2 + h * cut + c, give.at[1 - h, pieces[h][c]], take.at[1 - h, pieces[h][c]],
                    "seq", second[h]) for c in range(cut)] for h in range(2)]

    def start_far(h):
        for copy in far[h]:
            copy.start()

    def merge(h, c):
        far[h][c].wait_recv()

        def step(i, carry):
            rows = pl.ds(pl.multiple_of(h * half + c * size + i * 64, 64), 64)
            more = pl.ds(pl.multiple_of(c * size + i * 64, 64), 64)
            give[1 - h, rows, :] = (give[1 - h, rows, :].astype(jnp.float32)
                                    + transit[h, more, :].astype(jnp.float32)).astype(jnp.bfloat16)
            return carry

        lax.fori_loop(0, size // 64, step, 0)
        summed[h][c].start()

    def finish(h):
        plain[h].wait()
        for c in range(cut):
            summed[h][c].wait()
            far[h][c].wait_send()

    return start_far, (plain[0].start, plain[1].start), merge, finish


def middle_kernel(out_ref, x_ref, weight_in, gate_up_in, down_in, gains_ref, dy0_in, dy1_in, dy2_in, dy3_in,
                  hidden_out, branch0_out, branch1_out, branch2_out, branch3_out, grads_out, dh_out,
                  do_ref, gain_grad_ref, down_piece_ref,
                  raw_ref, tail_in, weight_ref, dy_ref, hidden_ref, branch_ref, grads_ref, mixed_ref, normed_ref, act_ref, dgu_ref,
                  give_ref, transit_ref, take_ref, own_ref, low_ref, do_give_ref, twin_ref, total_ref, shard_take_ref,
                  local_sem, send_sem, recv_sem):
    low = jnp.bfloat16
    rows, model = x_ref.shape
    width = out_ref.shape[1]
    units = act_ref.shape[2]
    early = units - TILE
    tail_at = model + 3 * early
    shard = tail_in.shape[0]
    count = model // shard
    mine, peers = seq_peers()
    px, py, _ = peers
    place, sibling, others = shard_peers(count)
    half = rows // 2
    halves = (pl.ds(0, half), pl.ds(half, half))
    whole = pl.ds(0, rows)
    send = sender(send_sem, recv_sem)
    local = starter(local_sem)
    branch_outs = (branch0_out, branch1_out, branch2_out, branch3_out)
    out_in = local(0, weight_in.at[:, :model], weight_ref.at[:, :model])
    feed_in = [local(1, weight_in.at[:, model:], weight_ref.at[:, model:tail_at])]
    feed_in += [local(2 + k, dy_in, dy_ref.at[k]) for k, dy_in in enumerate((dy0_in, dy1_in, dy2_in, dy3_in))]

    def tiles(amount, body, first=0):
        def step(i, carry):
            body(pl.multiple_of(i * TILE, TILE))
            return carry
        lax.fori_loop(first, first + amount // TILE, step, 0)

    def half_of(owner, h):
        return pl.ds(pl.multiple_of(owner * rows + h * half, half), half)

    ready = greet(peers, [sibling] + others)
    raw = [local(14 + b, weight.at[:, pl.ds(pl.multiple_of(at * units + early, TILE), TILE)],
                 raw_ref.at[:, pl.ds(b * TILE, TILE)])
           for b, (weight, at) in enumerate(((gate_up_in, mine), (gate_up_in, 4 + mine), (down_in, mine)))]
    for copy in raw:
        copy.wait()
    tail_in[...] = raw_ref[...].astype(low)
    mixed_ref[:, span(mine, width)] = out_ref[span(mine, rows), :]
    tail_ref = weight_ref.at[span(place, shard), tail_at:]
    tail_ref[...] = tail_in[...]
    ready()
    turn = [[send(3 * h + k, out_ref.at[half_of(peer, h), :], mixed_ref.at[halves[h], span(mine, width)], "seq", peer)
             for k, peer in enumerate(peers)] for h in range(2)]
    for h in range(2):
        for k in (2, 0, 1):
            turn[h][k].start()

    def tail_of(owner):
        return weight_ref.at[span(owner, shard), tail_at:]

    tails = [send(28 + k, tail_in, tail_of(place), "fsdp", peer) for k, peer in enumerate([sibling] + others)]
    for k in list(range(1, len(tails))) + [0]:
        tails[k].start()
    parts = [tail_of(lax.rem(place - 2 * k + count, count)) for k in range(1, len(tails))]
    twins = [send(29 + count // 2 + k, part, part, "fsdp", sibling) for k, part in enumerate(parts)]

    def pass_tail(k):
        tails[k].wait_recv()
        twins[k - 1].start()

    steps = [range(1 + (len(others) * t) // 3, 1 + (len(others) * (t + 1)) // 3) for t in range(3)]
    for copy in feed_in:
        copy.wait()

    def grad_act(down_at, dup_at):
        def step(slot, carry):
            dgu_ref[slot, :, pl.ds(dup_at, TILE)] = dot(dy_ref[slot], weight_ref[:, pl.ds(down_at, TILE)]).astype(low)
            return carry
        lax.fori_loop(0, 4, step, 0)

    tiles(early, lambda f: grad_act(model + 2 * early + f, early + f))
    x_sends = [send(6 + h, normed_ref.at[0, halves[h]], normed_ref.at[1, halves[h]], "seq", px) for h in range(2)]
    y_sends = [send(8 + h, normed_ref.at[0, halves[h]], normed_ref.at[2, halves[h]], "seq", py) for h in range(2)]
    x_relay = send(10, normed_ref.at[1, halves[0]], normed_ref.at[3, halves[0]], "seq", py)
    y_relay = send(11, normed_ref.at[2, halves[1]], normed_ref.at[3, halves[1]], "seq", px)
    for h in range(2):
        for k in range(3):
            turn[h][k].wait_recv()
        if h == 0:
            out_in.wait()

        def project(c, h=h):
            cols = pl.ds(c, TILE)
            hidden_ref[halves[h], cols] = x_ref[halves[h], cols].astype(jnp.float32) + dot(
                mixed_ref[halves[h], :], weight_ref[:, cols])

        tiles(model, project)

        def norm(i, carry, h=h):
            part = pl.ds(pl.multiple_of(h * half + i * 64, 64), 64)
            value = hidden_ref[part, :]
            normed_ref[0, part, :] = (value * rms_scale(value) * gains_ref[1:2, :]).astype(low)
            return carry

        lax.fori_loop(0, half // 64, norm, 0)
        x_sends[h].start()
        y_sends[h].start()
        for k in steps[h]:
            pass_tail(k)

    def unit_tile(slot, part, gate_at, up_at, act_at, dgate_at, dup_at):
        gate = dot(normed_ref[slot, part, :], weight_ref[:, pl.ds(gate_at, TILE)])
        up = dot(normed_ref[slot, part, :], weight_ref[:, pl.ds(up_at, TILE)])
        grad_act = dgu_ref[slot, part, pl.ds(dup_at, TILE)].astype(jnp.float32)
        sigmoid = jax.nn.sigmoid(gate)
        silu = gate * sigmoid
        act_ref[slot, part, pl.ds(act_at, TILE)] = (silu * up).astype(low)
        dgu_ref[slot, part, pl.ds(dgate_at, TILE)] = (
            grad_act * up * sigmoid * (1.0 + gate * (1.0 - sigmoid))).astype(low)
        dgu_ref[slot, part, pl.ds(dup_at, TILE)] = (grad_act * silu).astype(low)

    def feed(slot, part):
        def step(i, carry):
            is_tail = (i * TILE == early).astype(jnp.int32)
            f = i * TILE

            def at(usual, last):
                return pl.multiple_of(usual + is_tail * (last - usual), TILE)

            unit_tile(slot, part, at(model + f, tail_at), at(model + early + f, tail_at + TILE),
                      pl.multiple_of(f, TILE), at(f, 2 * early),
                      at(early + f, 2 * early + TILE))
            return carry
        lax.fori_loop(0, units // TILE, step, 0)

    def back(slot, part):
        def body(c):
            cols = pl.ds(c, TILE)
            value = dot(dgu_ref[slot, part, :2 * early], weight_ref[cols, model:model + 2 * early], NT) + dot(
                dgu_ref[slot, part, 2 * early:], weight_ref[cols, tail_at:tail_at + 2 * TILE], NT)

            if isinstance(slot, int):
                own_ref[part, cols] = value
            else:
                give_ref[slot - 1, part, cols] = value.astype(low)
        tiles(model, body)

    start_far, start_plain, merge, finish = collect(send, 12, give_ref, transit_ref, take_ref, peers, 2)
    outs = [local(6, hidden_ref, hidden_out)]
    for k in steps[2]:
        pass_tail(k)
    tails[0].wait_recv()
    for copy in twins:
        copy.wait_recv()
    grad_act(tail_at + 2 * TILE, 2 * early + TILE)
    unit_count = units // TILE

    def branch(i, carry):
        cols = pl.ds(pl.multiple_of(i % (model // TILE) * TILE, TILE), TILE)
        slot = i // (model // TILE)
        branch_ref[slot, :, cols] = (
            dot(act_ref[slot, :, :early], weight_ref[cols, model + 2 * early:tail_at], NT)
            + dot(act_ref[slot, :, early:], weight_ref[cols, tail_at + 2 * TILE:], NT)).astype(low)
        for k in range(4):
            @pl.when(i == (k + 1) * (model // TILE) - 1)
            def _():
                branch_copies[k].start()
        return carry

    branch_copies = [pltpu.make_async_copy(branch_ref.at[k], branch_outs[k], local_sem.at[(7, 10, 11, 12)[k]])
                     for k in range(4)]

    def work(i, carry):
        def flag(test):
            return test.astype(jnp.int32)

        slot = flag(i >= 2) + flag((i == 3) | (i == 4)) + 2 * flag(i >= 6)
        h = flag((i == 1) | (i == 4) | (i == 5) | (i == 7))
        part = pl.ds(pl.multiple_of(h * half, half), half)

        def on(index, *actions):
            @pl.when(i == index)
            def _():
                for action in actions:
                    action()

        on(2, x_sends[0].wait_recv, x_relay.start)
        on(3, y_sends[0].wait_recv)
        on(4, y_sends[1].wait_recv, y_relay.start)
        on(5, x_sends[1].wait_recv)
        @pl.when(i == 6)
        def _():
            lax.fori_loop(0, 2 * (model // TILE), branch, 0)

        on(6, x_relay.wait_recv)
        on(7, y_relay.wait_recv)
        feed(slot, part)
        back(slot, part)
        on(2, start_plain[0])
        on(4, start_plain[1])
        on(6, lambda: start_far(0))
        on(7, lambda: start_far(1))
        return carry

    feed(0, whole)
    back(0, whole)
    lax.fori_loop(2, 8, work, 0)

    def weight_grad(left_ref, right_ref, base, first, amount):
        def step(i, carry):
            part = pl.ds(pl.multiple_of(i % 2 * (model // 2), model // 2), model // 2)
            f = pl.multiple_of(i // 2 * TILE, TILE)
            acc = dot(left_ref[0, :, part], right_ref[0, :, pl.ds(f, TILE)], TN)
            for slot in range(1, 4):
                acc += dot(left_ref[slot, :, part], right_ref[slot, :, pl.ds(f, TILE)], TN)
            grads_ref[part, pl.ds(base + f, TILE)] = acc.astype(low)
            return carry
        lax.fori_loop(2 * first, 2 * (first + amount), step, 0)

    def gate_up_grad(first, amount):
        weight_grad(normed_ref, dgu_ref, 0, first, amount)

    down_cols = pl.ds(2 * units, units)

    shard_start, shard_pass, shard_finish = pair_sum(
        send, 28 + count, place, sibling, others, lambda part: grads_ref.at[part, down_cols],
        twin_ref, total_ref, shard_take_ref, shard)
    weight_grad(dy_ref, act_ref, 2 * units, 0, 2)
    merge(0, 0)
    merge(1, 0)
    weight_grad(dy_ref, act_ref, 2 * units, 2, unit_count - 2)
    merge(0, 1)
    merge(1, 1)
    shard_start()
    gate_up_grad(0, 5)
    shard_pass()
    gain_grad_ref[...] = jnp.zeros_like(gain_grad_ref)
    sends = [[send(22 + 3 * h + k, do_give_ref.at[k, halves[h]], do_ref.at[half_of(mine, h), :], "seq", peer)
              for k, peer in enumerate(peers)] for h in range(2)]
    for h in range(2):
        finish(h)

        def norm_back(i, carry, h=h):
            part = pl.ds(pl.multiple_of(h * half + i * 64, 64), 64)
            value = hidden_ref[part, :]
            inv = rms_scale(value)
            grad = own_ref[part, :] + take_ref[0, part, :].astype(jnp.float32) + take_ref[1, part, :].astype(jnp.float32)
            gain_grad_ref[0:1, :] += jnp.sum(grad * value * inv, axis=0, keepdims=True)
            scaled = grad * gains_ref[1:2, :]
            dh = dy_ref[0, part, :].astype(jnp.float32) + (
                inv * scaled - value * inv**3 * jnp.mean(value * scaled, axis=-1, keepdims=True))
            own_ref[part, :] = dh
            low_ref[part, :] = dh.astype(low)
            return carry

        lax.fori_loop(0, half // 64, norm_back, 0)
        for k in (2, 0, 1):
            do_give_ref[k, halves[h], :] = dot(
                low_ref[halves[h], :], weight_ref[span(peers[k], width), :model], NT).astype(low)
            sends[h][k].start()
        do_ref[half_of(mine, h), :] = dot(low_ref[halves[h], :], weight_ref[span(mine, width), :model], NT).astype(low)
    outs.append(local(8, own_ref, dh_out))
    gate_up_grad(5, 2 * units // TILE - 5)
    outs.append(local(9, grads_ref.at[:, :2 * units], grads_out.at[:, :2 * units]))

    def out_grad(c):
        cols = pl.ds(c, TILE)
        grads_ref[:, pl.ds(3 * units + c, TILE)] = dot(mixed_ref[...], low_ref[:, cols], TN).astype(low)

    tiles(model, out_grad)
    outs.append(local(13, grads_ref.at[:, 3 * units:], grads_out.at[:, 2 * units:]))

    lax.fori_loop(2 * (model // TILE), 4 * (model // TILE), branch, 0)
    outs += branch_copies
    shard_finish(down_piece_ref)
    for copy in outs:
        copy.wait()
    for copy in tails + twins:
        copy.wait_send()
    for h in range(2):
        x_sends[h].wait_send()
        y_sends[h].wait_send()
        for k in range(3):
            turn[h][k].wait_send()
            sends[h][k].wait()
    x_relay.wait_send()
    y_relay.wait_send()


def middle(dealt_out, x, weights, gate_up, down, gains, dy, units):
    low = jnp.bfloat16
    group_len, width = dealt_out.shape
    rows, model = x.shape
    shard = down.shape[0]
    count = model // shard
    f32 = jnp.float32
    shape = jax.ShapeDtypeStruct
    copies = 28 + 2 * count
    return pl.pallas_call(
        middle_kernel,
        name="middle",
        out_shape=(
            shape((rows, model), f32),
            *[shape((rows, model), low)] * 4,
            shape((model, 2 * units + model), low),
            shape((rows, model), f32),
            shape((group_len, width), low),
            shape((8, model), f32),
            shape((shard, units), low),
        ),
        in_specs=[vmem(), vmem(), hbm(), hbm(), hbm(), vmem()] + [hbm()] * 4,
        out_specs=(hbm(),) * 7 + (vmem(),) * 3,
        scratch_shapes=[
            pltpu.VMEM((shard, 3 * TILE), f32),
            pltpu.VMEM((shard, 3 * TILE), low),
            pltpu.VMEM((model, model + 3 * units), low),
            pltpu.VMEM((4, rows, model), low),
            pltpu.VMEM((rows, model), f32),
            pltpu.VMEM((4, rows, model), low),
            pltpu.VMEM((model, 3 * units + model), low),
            pltpu.VMEM((rows, model), low),
            pltpu.VMEM((4, rows, model), low),
            pltpu.VMEM((4, rows, units), low),
            pltpu.VMEM((4, rows, 2 * units), low),
            pltpu.VMEM((3, rows, model), low),
            pltpu.VMEM((2, rows // 2, model), low),
            pltpu.VMEM((2, rows, model), low),
            pltpu.VMEM((rows, model), f32),
            pltpu.VMEM((rows, model), low),
            pltpu.VMEM((3, rows, width), low),
            pltpu.VMEM((count // 2, shard, units), low),
            pltpu.VMEM((count // 2, shard, units), low),
            pltpu.VMEM((count // 2, shard, units), low),
            pltpu.SemaphoreType.DMA((17,)),
            pltpu.SemaphoreType.DMA((copies,)),
            pltpu.SemaphoreType.DMA((copies,)),
        ],
        compiler_params=pltpu.CompilerParams(
            vmem_limit_bytes=62 << 20, collective_id=1, has_side_effects=True),
        cost_estimate=pl.CostEstimate(flops=60_000_000_000, bytes_accessed=40 << 20, transcendentals=0),
    )(dealt_out, x, weights, gate_up, down, gains, *dy)


def gather_kernel(x_ref, all_ref, local_sem, send_sem, recv_sem):
    rows = x_ref.shape[0]
    mine, peers = seq_peers()
    send = sender(send_sem, recv_sem)
    half = rows // 2
    px, py, _ = peers

    def part(owner, h):
        return all_ref.at[pl.ds(pl.multiple_of(owner * rows + h * half, half), half)]

    ready = greet(peers)
    keep = pltpu.make_async_copy(x_ref, all_ref.at[span(mine, rows)], local_sem)
    keep.start()
    ready()
    x_sends = [send(h, x_ref.at[pl.ds(h * half, half)], part(mine, h), "seq", px) for h in range(2)]
    y_sends = [send(2 + h, x_ref.at[pl.ds(h * half, half)], part(mine, h), "seq", py) for h in range(2)]
    for copy in (x_sends[0], y_sends[1], x_sends[1], y_sends[0]):
        copy.start()
    x_relay = send(4, part(px, 0), part(px, 0), "seq", py)
    y_relay = send(5, part(py, 1), part(py, 1), "seq", px)
    x_sends[0].wait_recv()
    x_relay.start()
    y_sends[1].wait_recv()
    y_relay.start()
    x_sends[1].wait_recv()
    y_sends[0].wait_recv()
    for copy in x_sends + y_sends:
        copy.wait_send()
    x_relay.wait()
    y_relay.wait()
    keep.wait()


def gather_rows(x):
    rows, model = x.shape
    return pl.pallas_call(
        gather_kernel,
        name="gather_rows",
        out_shape=jax.ShapeDtypeStruct((4 * rows, model), x.dtype),
        in_specs=[hbm()],
        out_specs=hbm(),
        scratch_shapes=[
            pltpu.SemaphoreType.DMA,
            pltpu.SemaphoreType.DMA((6,)),
            pltpu.SemaphoreType.DMA((6,)),
        ],
        compiler_params=pltpu.CompilerParams(collective_id=0, has_side_effects=True),
        cost_estimate=pl.CostEstimate(flops=40_000_000_000, bytes_accessed=20 << 20, transcendentals=0),
    )(x)


def rear_kernel(grad_ref, normed_in, slab_ref, gains_ref, x_in, dh_in, hidden_in, branch0_in, branch1_in, branch2_in,
                branch3_in, result_out, input_grad_out, gain_grad_ref, piece_ref,
                result_ref, input_grad_ref, normed_ref, x_ref, dh_ref, hidden_ref, branch_ref, give_ref, transit_ref, take_ref, own_ref, term_ref,
                twin_ref, total_ref, shard_take_ref, local_sem, send_sem, recv_sem):
    low = jnp.bfloat16
    rows, model = result_ref.shape
    shard, columns = piece_ref.shape
    count = model // shard
    half = rows // 2
    mine, peers = seq_peers()
    place, sibling, others = shard_peers(count)
    send = sender(send_sem, recv_sem)
    local = starter(local_sem)
    normed_copy = local(0, normed_in, normed_ref)
    row_copies = [local(1, x_in, x_ref), local(2, dh_in, dh_ref)]
    result_copies = [local(3, hidden_in, hidden_ref)]
    result_copies.append(local(4, branch0_in, branch_ref))

    def partial(owner, first, amount, store):
        block = pl.ds(pl.multiple_of(owner * rows + first, half), amount)

        def body(i, carry):
            cols = pl.ds(pl.multiple_of(i * TILE, TILE), TILE)
            store(cols, dot(grad_ref[block, :], slab_ref[cols, :columns], NT))
            return carry

        lax.fori_loop(0, model // TILE, body, 0)

    def hand(k, first, amount):
        def store(cols, value):
            give_ref[k, pl.ds(first, amount), cols] = value.astype(low)
        partial(peers[k], first, amount, store)

    def keep(cols, value):
        own_ref[:, cols] = value

    ready = greet(peers, [sibling] + others)
    hand(2, 0, half)
    ready()
    start_far, start_plain, merge, finish = collect(send, 0, give_ref, transit_ref, take_ref, peers, 2)
    start_far(0)
    hand(2, half, half)
    start_far(1)
    for h in range(2):
        hand(h, 0, rows)
        start_plain[h]()

    def weight_term(i, carry):
        part = pl.ds(pl.multiple_of(i * TILE, TILE), TILE)
        term_ref[part, :] = dot(normed_ref[:, part], grad_ref[...], TN).astype(low)
        return carry

    normed_copy.wait()
    lax.fori_loop(0, model // TILE, weight_term, 0)
    shard_start, shard_pass, shard_finish = pair_sum(
        send, 10, place, sibling, others, lambda part: term_ref.at[part], twin_ref, total_ref, shard_take_ref, shard)
    shard_start()
    for c in range(2):
        for h in range(2):
            merge(h, c)
    shard_pass()
    partial(mine, 0, rows, keep)
    for copy in result_copies:
        copy.wait()

    def result(i, carry):
        part = pl.ds(pl.multiple_of(i * 64, 64), 64)
        value = hidden_ref[part, :]
        for piece in (branch_ref, branch1_in, branch2_in, branch3_in):
            value += piece[part, :].astype(jnp.float32)
        result_ref[part, :] = value.astype(low)
        return carry

    lax.fori_loop(0, rows // 64, result, 0)
    outs = [local(8, result_ref, result_out)]
    for copy in row_copies:
        copy.wait()
    gain_grad_ref[...] = jnp.zeros_like(gain_grad_ref)

    def norm_back(i, carry):
        part = pl.ds(pl.multiple_of(i * 64, 64), 64)
        x = x_ref[part, :].astype(jnp.float32)
        inv = rms_scale(x)
        grad = own_ref[part, :] + take_ref[0, part, :].astype(jnp.float32) + take_ref[1, part, :].astype(jnp.float32)
        gain_grad_ref[0:1, :] += jnp.sum(grad * x * inv, axis=0, keepdims=True)
        scaled = grad * gains_ref[0:1, :]
        input_grad_ref[part, :] = (dh_ref[part, :] + (
            inv * scaled - x * inv**3 * jnp.mean(x * scaled, axis=-1, keepdims=True))).astype(low)
        return carry

    for h in range(2):
        finish(h)
        lax.fori_loop(h * half // 64, (h + 1) * half // 64, norm_back, 0)
        part = pl.ds(h * half, half)
        outs.append(local(9 + h, input_grad_ref.at[part], input_grad_out.at[part]))
    shard_finish(piece_ref)
    for copy in outs:
        copy.wait()


def rear(grad, normed, slab, gains, x, dh, hidden, branch, shard):
    low = jnp.bfloat16
    f32 = jnp.float32
    rows, model = x.shape
    group_len, columns = grad.shape
    count = model // shard
    shape = jax.ShapeDtypeStruct
    copies = 10 + count
    return pl.pallas_call(
        rear_kernel,
        name="rear",
        out_shape=(shape((rows, model), low), shape((rows, model), low), shape((8, model), f32),
                   shape((shard, columns), low)),
        in_specs=[vmem(), hbm(), vmem(), vmem()] + [hbm()] * 4 + [vmem()] * 3,
        out_specs=(hbm(), hbm(), vmem(), vmem()),
        scratch_shapes=[
            pltpu.VMEM((rows, model), low),
            pltpu.VMEM((rows, model), low),
            pltpu.VMEM((group_len, model), low),
            pltpu.VMEM((rows, model), low),
            pltpu.VMEM((rows, model), f32),
            pltpu.VMEM((rows, model), f32),
            pltpu.VMEM((rows, model), low),
            pltpu.VMEM((3, rows, model), low),
            pltpu.VMEM((2, rows // 2, model), low),
            pltpu.VMEM((2, rows, model), low),
            pltpu.VMEM((rows, model), f32),
            pltpu.VMEM((model, columns), low),
            pltpu.VMEM((count // 2, shard, columns), low),
            pltpu.VMEM((count // 2, shard, columns), low),
            pltpu.VMEM((count // 2, shard, columns), low),
            pltpu.SemaphoreType.DMA((11,)),
            pltpu.SemaphoreType.DMA((copies,)),
            pltpu.SemaphoreType.DMA((copies,)),
        ],
        compiler_params=pltpu.CompilerParams(
            vmem_limit_bytes=56 << 20, collective_id=2, has_side_effects=True),
        cost_estimate=pl.CostEstimate(flops=50_000_000_000, bytes_accessed=20 << 20, transcendentals=0),
    )(grad, normed, slab, gains, x, dh, hidden, *branch)


def last_kernel(pieces_ref, qkv_ref, down_ref, gain_a_ref, gain_b_ref, out_qkv_ref, out_out_ref, out_gate_up_ref, out_down_ref,
                gains_ref, block_ref, slots_ref, gain_own_ref, gain_take_ref, gain_slots_ref, local_sem, send_sem, recv_sem):
    low = jnp.bfloat16
    shard, columns = qkv_ref.shape
    model = gain_a_ref.shape[1]
    count = model // shard
    units = out_down_ref.shape[1] // 4
    width = columns // 3
    mine, peers = seq_peers()
    place, sibling, _ = shard_peers(count)
    everyone = [lax.rem(place + k, count) for k in range(1, count)]
    send = sender(send_sem, recv_sem)
    ready = greet(peers, everyone)
    local = starter(local_sem)
    fills = [local(0, qkv_ref, block_ref.at[:, :columns]), local(1, down_ref, block_ref.at[:, columns:columns + units]),
             local(2, pieces_ref, block_ref.at[:, columns + units:])]
    gain_own_ref[0:1, :] = gain_a_ref[0:1, :]
    gain_own_ref[1:2, :] = gain_b_ref[0:1, :]
    gain_own_ref[2:8, :] = jnp.zeros((6, model), jnp.float32)
    for copy in fills:
        copy.wait()
    ready()
    forward, arrivals, finish = spread(send, 0, block_ref, [slots_ref.at[k] for k in range(3)], peers)
    gain_sends = [send(6 + k, gain_own_ref, gain_take_ref.at[k], "fsdp", peer) for k, peer in enumerate(everyone)]
    for copy in gain_sends:
        copy.start()

    def place_block(source, owner, first):
        for b in range(3):
            out_qkv_ref[:, span(b * 4 + owner, width)] = source[:, b * width:(b + 1) * width]
        out_down_ref[:, span(owner, units)] = source[:, columns:columns + units]
        at = columns + units
        for shift, size in ((0, units - TILE), (units - TILE, TILE)):
            for b in range(2):
                out_gate_up_ref[:, pl.ds(pl.multiple_of((b * 4 + owner) * units + shift, TILE), size)] = (
                    source[:, at:at + size])
                at += size
        if first:
            out_out_ref[...] = source[:, at:].astype(jnp.float32)
        else:
            out_out_ref[...] += source[:, at:].astype(jnp.float32)

    place_block(block_ref, mine, True)
    forward()
    total = gain_own_ref[...]
    for k, copy in enumerate(gain_sends):
        copy.wait_recv()
        total += gain_take_ref[k]
    gains_ref[...] = total
    seq_sends = [send(6 + len(everyone) + k, gains_ref, gain_slots_ref.at[k], "seq", peer) for k, peer in enumerate(peers)]
    for copy in seq_sends:
        copy.start()
    for k in range(3):
        arrivals[k]()
        place_block(slots_ref.at[k], peers[k], False)
    for copy in seq_sends:
        copy.wait()
    gains_ref[...] += gain_slots_ref[0] + gain_slots_ref[1] + gain_slots_ref[2]
    for copy in gain_sends:
        copy.wait_send()
    finish()


def last(pieces, qkv_piece, down_piece, gain_a, gain_b, units):
    low = jnp.bfloat16
    shard, columns = qkv_piece.shape
    model = gain_a.shape[1]
    count = model // shard
    f32 = jnp.float32
    shape = jax.ShapeDtypeStruct
    wide = columns + units + pieces.shape[1]
    copies = 9 + count
    return pl.pallas_call(
        last_kernel,
        name="last",
        out_shape=(
            shape((shard, 4 * columns), low),
            shape((shard, model), f32),
            shape((shard, 8 * units), low),
            shape((shard, 4 * units), low),
            shape((8, model), f32),
        ),
        in_specs=[hbm()] * 3 + [vmem()] * 2,
        out_specs=(vmem(),) * 5,
        scratch_shapes=[
            pltpu.VMEM((shard, wide), low),
            pltpu.VMEM((3, shard, wide), low),
            pltpu.VMEM((8, model), f32),
            pltpu.VMEM((count - 1, 8, model), f32),
            pltpu.VMEM((3, 8, model), f32),
            pltpu.SemaphoreType.DMA((3,)),
            pltpu.SemaphoreType.DMA((copies,)),
            pltpu.SemaphoreType.DMA((copies,)),
        ],
        compiler_params=pltpu.CompilerParams(
            vmem_limit_bytes=40 << 20, collective_id=3, has_side_effects=True),
        cost_estimate=pl.CostEstimate(flops=40_000_000_000, bytes_accessed=20 << 20, transcendentals=0),
    )(pieces, qkv_piece, down_piece, gain_a, gain_b)


def widen_kernel(*refs):
    for source, target in zip(refs[:6], refs[6:]):
        target[...] = source[...].astype(target.dtype)


def widen(shard, arrays):
    steps = max(shard // 32, 1)
    specs = [pl.BlockSpec((array.shape[0] // steps, array.shape[1]), lambda i: (i, 0)) for array in arrays]
    return pl.pallas_call(
        widen_kernel,
        name="widen",
        grid=(steps,),
        out_shape=[jax.ShapeDtypeStruct(array.shape, jnp.float32 if array.shape[0] == shard else array.dtype)
                   for array in arrays],
        in_specs=specs,
        out_specs=specs,
        compiler_params=pltpu.CompilerParams(vmem_limit_bytes=40 << 20),
    )(*arrays)


def swaps(rows):
    return [lax.ppermute(piece, "seq", table) for piece, table in zip(
        rows, ([(i, i ^ 1) for i in range(4)], [(i, (i + 2) % 4) for i in range(4)], [(i, 3 - i) for i in range(4)]))]


def on_device(block_input, norm_gain_a, weight_qkv, weight_out, norm_gain_b, weight_gate_up, weight_down,
              cotangent, permutation, lengths, offsets):
    low = jnp.bfloat16
    f32 = jnp.float32
    seq_count = lax.axis_size("seq")
    mine = lax.axis_index("seq")
    row_count, model_width = block_input.shape[1:]
    group_len = row_count * seq_count
    shard = weight_qkv.shape[0]
    head_width = weight_qkv.shape[1] // 3 // seq_count
    part_units = weight_down.shape[1] // seq_count
    perm = permutation[0]
    offs = offsets[0]
    position = jnp.arange(group_len, dtype=jnp.int32)
    start = jnp.max(jnp.where(offs[None, :] <= position[:, None], offs[None, :], 0), axis=1)

    def columns(weight, width, first, amount):
        blocks = weight.shape[1] // (seq_count * width)
        return [lax.dynamic_slice_in_dim(weight, (b * seq_count + mine) * width + first, amount, axis=1).astype(low)
                for b in range(blocks)]

    def gather_weight(parts):
        return lax.all_gather(jnp.concatenate(parts, axis=1), "fsdp", axis=0, tiled=True)

    early = part_units - TILE
    gain_cols = jnp.pad(jnp.stack([norm_gain_a, norm_gain_b], axis=1).astype(low), ((0, 0), (0, 126)))
    slab = gather_weight(columns(weight_qkv, head_width, 0, head_width) + [gain_cols])
    weights = gather_weight([weight_out.astype(low)] + columns(weight_gate_up, part_units, 0, early)
                            + columns(weight_down, part_units, 0, early))
    rows_all = gather_rows(block_input[0])
    grad_own, rows_all = lax.optimization_barrier((cotangent[0], rows_all))
    grad_rows = [cotangent[0]] + swaps([grad_own] * 3)
    ordered, dealt_out, wide_out, log_total, normed_a, gains = attention_forward(offs, rows_all, slab, perm, start)
    hidden, branch0, branch1, branch2, branch3, grads, grad_hidden, grad_heads, gain_b_term, down_piece = middle(
        dealt_out, block_input[0], weights, weight_gate_up, weight_down, gains, grad_rows, part_units)
    pieces = lax.psum_scatter(grads, "fsdp", scatter_dimension=0, tiled=True)
    branch = [branch0] + swaps([branch1, branch2, branch3])
    dealt_grad = attention_backward(offs, grad_heads, ordered, perm, start, wide_out, log_total)
    result_rows, input_grad, gain_a_term, qkv_piece = rear(
        dealt_grad, normed_a, slab, gains, block_input[0], grad_hidden, hidden, branch, shard)
    grad_qkv, grad_out, grad_gate_up, grad_down, gain_terms = last(
        pieces, qkv_piece, down_piece, gain_a_term, gain_b_term, part_units)
    gain_terms = lax.dynamic_slice_in_dim(gain_terms, lax.axis_index("fsdp") * shard, shard, axis=1)
    grad_qkv, grad_out, grad_gate_up, grad_down, result_rows, input_grad = widen(
        shard, [grad_qkv, grad_out, grad_gate_up, grad_down, result_rows, input_grad])
    return (
        result_rows[None],
        input_grad[None],
        gain_terms[0],
        grad_qkv,
        grad_out,
        gain_terms[1],
        grad_gate_up,
        grad_down,
    )


def solution(mesh):
    rows = P("fsdp", "seq", None)
    vector = P("fsdp")
    matrix = P("fsdp", None)
    return jax.shard_map(
        on_device,
        mesh=mesh,
        in_specs=(rows, vector, matrix, matrix, vector, matrix, matrix, rows, matrix, matrix, matrix),
        out_specs=(rows, rows, vector, matrix, matrix, vector, matrix, matrix),
        check_vma=False,
    )
```

profile of v0, /device:TPU:0, one launch (start us, length us, event | category | flops | bytes accessed | tf_op | source)
XLA Modules:
  0.0 381.5 jit_solution(3383201530808957114)
XLA Ops:
  7.2 0.0 all-gather.3.cloned.1.call-start
  7.2 0.7 convert_bitcast_fusion
  7.9 0.1 copy.27
  8.1 1.1 dynamic-slice_convert_fusion.5
  9.1 0.7 fusion.1
  9.8 0.0 all-gather.3.cloned.1.call-update
  9.8 0.0 all-gather.5.cloned.1.call-start
  9.9 1.1 convert_element_type.27
  11.0 1.3 dynamic-slice_convert_fusion.2
  12.3 1.0 pad_maximum_fusion
  13.2 0.0 all-gather.5.cloned.1.call-update
  13.3 0.0 reduce-scatter.2.cloned.1.call-start
  13.3 0.0 copy-start.15
  13.3 0.0 copy-start.2
  13.3 0.0 copy-start.3
  13.4 39.0 %gather_rows.1.x_ref = bf16[2048,1024]{1,0:T(8,128)(2,1)} custom-call(bf16[512,1024]{1,0:T(8,128)(2,1)} %bitcast.25), custom_call_target="tpu_custom_call" | custom-call | flops 40000000000 | bytes 20971520 | tf_op jit(solution)/shard_map/gather_rows/pallas_call | solution.py:809
  52.4 1.5 collective-permute-start.2
  53.9 1.5 collective-permute-start.1
  55.4 0.6 collective-permute-start
  56.0 0.4 copy.28.perm_col_ref
  56.4 0.1 select_reduce_fusion
  56.5 0.0 all-gather.3.cloned.1.call-done.slab_ref
  56.5 1.5 copy-done.4
  58.0 47.9 %attention_forward.1 = (bf16[2048,768]{1,0:T(8,128)(2,1)}, bf16[2048,256]{1,0:T(8,128)(2,1)S(1)}, f32[256,2048]{1,0:T(8,128)S(1)}, f32[8,2048]{1,0:T(8,128)S(1)}...) custom-call(s32[3]{0:T(128)S(1)} %bitcast.19, bf16[2048,1024]{1,0:T(8,128)(2,1)} %gather_rows.1.x_ref, ...), custom_call_target="tpu_custom_call" | custom-call | flops 24000000000 | bytes 16777216 | tf_op jit(solution)/shard_map/attention_forward/pallas_call | solution.py:231
  105.9 0.0 copy-start.6
  105.9 1.3 copy-done.6
  107.2 1.0 copy-done.8
  108.2 0.6 copy-done.12
  108.8 1.9 all-gather.5.cloned.1.call-done.weight_in
  110.8 114.5 %middle.1 = (f32[512,1024]{1,0:T(8,128)}, bf16[512,1024]{1,0:T(8,128)(2,1)}, bf16[512,1024]{1,0:T(8,128)(2,1)}, bf16[512,1024]{1,0:T(8,128)(2,1)}, bf16[512,1024...) custom-call(bf16[2048,256]{1,0:T(8,128)(2,1)} %copy-done.8, ...), custom_call_target="tpu_custom_call" | custom-call | flops 60000002048 | bytes 41943040 | tf_op jit(solution)/shard_map/middle/pallas_call | solution.py:729
  225.3 0.0 reduce-scatter.2.cloned.1.call-update
  225.3 0.1 collective-permute-start.3
  225.4 1.3 collective-permute-start.4
  226.7 2.2 collective-permute-start.5
  228.9 1.6 copy-done.7
  230.5 37.5 %attention_backward.1.grad_ref = bf16[2048,768]{1,0:T(8,128)(2,1)} custom-call(s32[3]{0:T(128)S(1)} %bitcast.20, bf16[2048,256]{1,0:T(8,128)(2,1)S(1)} %copy-done.9, bf16[2048,768]{1,0:T(8,128)(2,1)} %get-tuple-element.47.sorted_in, s32[1,2048]{1,0:T(1,128)S(1)} %copy-done.2, s32[2048,1]{1,0:T(8,128)S(1)} %copy.28.perm_col_ref, s32[1,2048]{1,0:T(1,128)S(1)} %bitcast.17, ...), custom_call_target="tpu_custom_call" | custom-call | flops 40000000000 | bytes 16777216 | tf_op jit(solution)/shard_map/attention_backward/pallas_call | solution.py:263
  268.0 0.0 copy-start.16
  268.1 2.8 collective-permute-done.4.branch2_in
  270.9 1.0 copy-done.17
  271.9 0.3 copy-done.18
  272.2 48.6 %rear.1 = (bf16[512,1024]{1,0:T(8,128)(2,1)}, bf16[512,1024]{1,0:T(8,128)(2,1)}, f32[8,1024]{1,0:T(8,128)}, bf16[128,768]{1,0:T(8,128)(2,1)}) custom-call(bf16[2048,768]{1,0:T(8,128)(2,1)} %attention_backward.1.grad_ref, bf16[2048,1024]{1,0:T(8,128)(2,1)} %get-tuple-element.50.normed_in, bf16[1024,896]{1,0:T(8,128)(2,1)} %all-gather.3.cloned.1.call-done.slab_ref, ...), custom_call_target="tpu_custom_call" | custom-call | flops 49999998976 | bytes 20971520 | tf_op jit(solution)/shard_map/rear/pallas_call | solution.py:933
  320.9 0.0 reduce-scatter.2.cloned.1.call-done.pieces_ref
  320.9 1.1 copy-done.5
  322.0 0.9 copy-done.11
  323.0 0.8 copy-done.14
  323.7 46.5 %last.1 = (bf16[128,3072]{1,0:T(8,128)(2,1)S(1)}, f32[128,1024]{1,0:T(8,128)S(1)}, bf16[128,8192]{1,0:T(8,128)(2,1)S(1)}, bf16[128,4096]{1,0:T(8,128)(2,1)S(1)}, f32[8,1024]{1,0:T(8,128)S(1)}) custom-call(bf16[128,3072]{1,0:T(8,128)(2,1)S(1)} %copy-done.5, bf16[128,768]{1,0:T(8,128)(2,1)S(1)} %copy-done.11, bf16[128,1024]{1,0:T(8,128)(2,1)S(1)} %copy-done.10, ...), custom_call_target="tpu_custom_call" | custom-call | flops 40000000000 | bytes 20971520 | tf_op jit(solution)/shard_map/last/pallas_call | solution.py:1038
  370.3 0.5 slice_bitcast_fusion
  370.8 4.1 %widen.1 = (f32[128,3072]{1,0:T(8,128)}, f32[128,1024]{1,0:T(8,128)}, f32[128,8192]{1,0:T(8,128)}, f32[128,4096]{1,0:T(8,128)}, bf16[512,1024]{1,0:T(8,128)(2,1)}, /*index=5*/bf16[512,1024]{1,0:T(8,128)(2,1)}) custom-call(bf16[128,3072]{1,0:T(8,128)(2,1)S(1)} %get-tuple-element.61.refs_0_, f32[128,1024]{1,0:T(8,128)S(1)} %get-tuple-element.62.refs_1_, ...), custom_call_target="tpu_custom_call" | custom-call | tf_op jit(solution)/shard_map/widen/pallas_call | solution.py:1074
  (30 shorter events, 0.1 us)
Async XLA Ops:
  7.2 49.3 %all-gather.3.cloned.1.call-start = ((), (), s32[]{:S(2)}) async-start(), calls=%async_computation.1 | async-start | bytes 2064384 | tf_op jit(solution)/shard_map/all_gather | solution.py:1113
  9.8 100.9 %all-gather.5.cloned.1.call-start = ((), (), s32[]{:S(2)}) async-start(), calls=%async_computation.2 | async-start | bytes 7667712 | tf_op jit(solution)/shard_map/all_gather | solution.py:1113
  13.3 307.6 %reduce-scatter.2.cloned.1.call-start = ((), (), s32[]{:S(2)}) async-start(), calls=%async_computation.3 | async-start | bytes 7077888 | tf_op jit(solution)/shard_map/reduce_scatter | solution.py:1126
  13.3 39.1 %copy-start.15 = (bf16[1,512,1024]{2,1,0:T(8,128)(2,1)S(1)}, bf16[1,512,1024]{2,1,0:T(8,128)(2,1)}, u32[]{:S(2)}) copy-start(bf16[1,512,1024]{2,1,0:T(8,128)(2,1)} %param.18) | copy-start | bytes 3145732
  13.3 42.6 %copy-start.2 = (s32[1,2048]{1,0:T(1,128)S(1)}, s32[1,2048]{1,0:T(1,128)}, u32[]{:S(2)}) copy-start(s32[1,2048]{1,0:T(1,128)} %perm_row_ref.3) | copy-start | bytes 24580
  13.3 43.0 %copy-start.3 = (s32[1,3]{1,0:T(1,128)S(1)}, s32[1,3]{1,0:T(1,128)}, u32[]{:S(2)}) copy-start(s32[1,3]{1,0:T(1,128)} %param.20) | copy-start | bytes 40
  52.4 56.4 %collective-permute-start.2 = (bf16[512,1024]{1,0:T(8,128)(2,1)S(1)}, bf16[512,1024]{1,0:T(8,128)(2,1)}, u32[]{:S(2)}, u32[]{:S(2)}) collective-permute-start(bf16[512,1024]{1,0:T(8,128)(2,1)S(1)} %bitcast.22), channel_id=1, source_target_pairs={{0,24},{8,16},{16,8},{24,0},{1,25},{9,17},{17,9},{25,1},{2,26},{10... | collective-permute-start | bytes 3145736 | tf_op jit(solution)/shard_map/ppermute | solution.py:1087
  53.9 54.9 %collective-permute-start.1 = (bf16[512,1024]{1,0:T(8,128)(2,1)S(1)}, bf16[512,1024]{1,0:T(8,128)(2,1)}, u32[]{:S(2)}, u32[]{:S(2)}) collective-permute-start(bf16[512,1024]{1,0:T(8,128)(2,1)S(1)} %bitcast.23), channel_id=1, source_target_pairs={{0,16},{8,24},{16,0},{24,8},{1,17},{9,25},{17,1},{25,9},{2,18},{10... | collective-permute-start | bytes 3145736 | tf_op jit(solution)/shard_map/ppermute | solution.py:1087
  55.4 53.4 %collective-permute-start = (bf16[512,1024]{1,0:T(8,128)(2,1)S(1)}, bf16[512,1024]{1,0:T(8,128)(2,1)}, u32[]{:S(2)}, u32[]{:S(2)}) collective-permute-start(bf16[512,1024]{1,0:T(8,128)(2,1)S(1)} %bitcast.24), channel_id=1, source_target_pairs={{0,8},{8,0},{16,24},{24,16},{1,9},{9,1},{17,25},{25,17},{2,10},{10... | collective-permute-start | bytes 3145736 | tf_op jit(solution)/shard_map/ppermute | solution.py:1087
  56.5 1.5 copy-start.4
  105.9 1.3 copy-start.6
  107.2 1.0 copy-start.8
  108.2 0.6 copy-start.12
  225.3 3.6 copy-start.9
  225.3 42.7 %collective-permute-start.3 = (bf16[512,1024]{1,0:T(8,128)(2,1)}, bf16[512,1024]{1,0:T(8,128)(2,1)S(1)}, u32[]{:S(2)}, u32[]{:S(2)}) collective-permute-start(bf16[512,1024]{1,0:T(8,128)(2,1)} %get-tuple-element.54), channel_id=1, source_target_pairs={{0,8},{8,0},{16,24},{24,16},{1,9},{9,1},{17,25},{25,17},{2,10},{10... | collective-permute-start | bytes 3145736 | tf_op jit(solution)/shard_map/ppermute | solution.py:1087
  225.4 45.5 %collective-permute-start.4 = (bf16[512,1024]{1,0:T(8,128)(2,1)}, bf16[512,1024]{1,0:T(8,128)(2,1)S(1)}, u32[]{:S(2)}, u32[]{:S(2)}) collective-permute-start(bf16[512,1024]{1,0:T(8,128)(2,1)} %get-tuple-element.55), channel_id=1, source_target_pairs={{0,16},{8,24},{16,0},{24,8},{1,17},{9,25},{17,1},{25,9},{2,18},{10... | collective-permute-start | bytes 3145736 | tf_op jit(solution)/shard_map/ppermute | solution.py:1087
  226.7 44.2 %collective-permute-start.5 = (bf16[512,1024]{1,0:T(8,128)(2,1)}, bf16[512,1024]{1,0:T(8,128)(2,1)S(1)}, u32[]{:S(2)}, u32[]{:S(2)}) collective-permute-start(bf16[512,1024]{1,0:T(8,128)(2,1)} %get-tuple-element.56), channel_id=1, source_target_pairs={{0,24},{8,16},{16,8},{24,0},{1,25},{9,17},{17,9},{25,1},{2,26},{10... | collective-permute-start | bytes 3145736 | tf_op jit(solution)/shard_map/ppermute | solution.py:1087
  228.9 1.6 copy-start.7
  268.0 2.9 copy-start.16
  270.9 1.0 copy-start.17
  270.9 1.3 copy-start.18
  272.2 48.7 %copy-start.10 = (bf16[128,1024]{1,0:T(8,128)(2,1)S(1)}, bf16[128,1024]{1,0:T(8,128)(2,1)}, u32[]{:S(2)}) copy-start(bf16[128,1024]{1,0:T(8,128)(2,1)} %get-tuple-element.58.down_ref) | copy-start | bytes 786436
  272.2 48.7 %copy-start.13 = (f32[8,1024]{1,0:T(8,128)S(1)}, f32[8,1024]{1,0:T(8,128)}, u32[]{:S(2)}) copy-start(f32[8,1024]{1,0:T(8,128)} %get-tuple-element.60.gain_b_ref) | copy-start | bytes 98308
  320.9 1.1 copy-start.5
  322.0 0.9 copy-start.11
  323.0 0.8 copy-start.14
  323.7 47.1 %copy-start = (bf16[512,1024]{1,0:T(8,128)(2,1)S(1)}, bf16[512,1024]{1,0:T(8,128)(2,1)}, u32[]{:S(2)}) copy-start(bf16[512,1024]{1,0:T(8,128)(2,1)} %get-tuple-element.65.refs_4_) | copy-start | bytes 3145732
  323.7 47.1 %copy-start.1 = (bf16[512,1024]{1,0:T(8,128)(2,1)S(1)}, bf16[512,1024]{1,0:T(8,128)(2,1)}, u32[]{:S(2)}) copy-start(bf16[512,1024]{1,0:T(8,128)(2,1)} %get-tuple-element.66.refs_5_) | copy-start | bytes 3145732
Sparse Core Ops, SparseCore 0:
  10.2 29.6 all-gather.2
  42.1 68.6 all-gather.4
  225.5 70.0 reduce-scatter.1
where the time goes:
time: 382 us; the launch traced here: 381 us
  Pallas kernels  338 us (88%)
  between operations  14 us (4%)
  local copies, waits for them, and re-layouts  13.5 us (4%)
  starting transfers between devices  7.22 us (2%)
  waiting for transfers between devices  4.88 us (1%)
    pallas_call x1, Pallas kernels, middle(): pl.pallas_call(middle_kernel, name='middle', out_shape=(shape((rows, mode...  115 us
    pallas_call x1, Pallas kernels, rear(): pl.pallas_call(rear_kernel, name='rear', out_shape=(shape((rows, model),...  48.6 us
    pallas_call x1, Pallas kernels, attention_forward(): pl.pallas_call(forward_kernel, name='attention_forward', out_shape=(shape...  47.9 us
    pallas_call x1, Pallas kernels, last(): pl.pallas_call(last_kernel, name='last', out_shape=(shape((shard, 4 * col...  46.5 us
    pallas_call x1, Pallas kernels, gather_rows(): pl.pallas_call(gather_kernel, name='gather_rows', out_shape=jax.ShapeDtyp...  39 us
    pallas_call x1, Pallas kernels, attention_backward(): pl.pallas_call(backward_kernel, name='attention_backward', out_shape=jax....  37.5 us
    unnamed x38, local copies, waits for them, and re-layouts  10.2 us
  transfers between devices with their start and end apart: 9, of which 2 were waited for; matrix products, arithmetic and copies ran while one was open for 1% of the time, Pallas kernels for 45%

commit v1 on v0

--- a/solution.py
+++ b/solution.py
@@ -252,7 +252,7 @@
             pltpu.SemaphoreType.DMA((3,)),
             pltpu.SemaphoreType.DMA((group_len // BLK,)),
         ],
-        compiler_params=pltpu.CompilerParams(vmem_limit_bytes=48 << 20),
+        compiler_params=pltpu.CompilerParams(vmem_limit_bytes=62 << 20),
         cost_estimate=pl.CostEstimate(flops=24_000_000_000, bytes_accessed=16 << 20, transcendentals=0),
     )(offs, rows, slab, perm.reshape(1, group_len), perm.reshape(group_len, 1), start.reshape(1, group_len))
 
@@ -279,7 +279,7 @@
             pltpu.SemaphoreType.DMA((2,)),
             pltpu.SemaphoreType.DMA((group_len // BLK,)),
         ],
-        compiler_params=pltpu.CompilerParams(vmem_limit_bytes=48 << 20),
+        compiler_params=pltpu.CompilerParams(vmem_limit_bytes=62 << 20),
         cost_estimate=pl.CostEstimate(flops=40_000_000_000, bytes_accessed=16 << 20, transcendentals=0),
     )(offs, grad, ordered, perm.reshape(1, group_len), perm.reshape(group_len, 1), start.reshape(1, group_len), wide, lse)
 
@@ -838,7 +838,8 @@
     normed_copy = local(0, normed_in, normed_ref)
     row_copies = [local(1, x_in, x_ref), local(2, dh_in, dh_ref)]
     result_copies = [local(3, hidden_in, hidden_ref)]
-    result_copies.append(local(4, branch0_in, branch_ref))
+    result_copies += [local(4 + k, piece, branch_ref.at[k])
+                      for k, piece in enumerate((branch0_in, branch1_in, branch2_in, branch3_in))]
 
     def partial(owner, first, amount, store):
         block = pl.ds(pl.multiple_of(owner * rows + first, half), amount)
@@ -890,8 +891,8 @@
     def result(i, carry):
         part = pl.ds(pl.multiple_of(i * 64, 64), 64)
         value = hidden_ref[part, :]
-        for piece in (branch_ref, branch1_in, branch2_in, branch3_in):
-            value += piece[part, :].astype(jnp.float32)
+        for k in range(4):
+            value += branch_ref[k, part, :].astype(jnp.float32)
         result_ref[part, :] = value.astype(low)
         return carry
 
@@ -935,7 +936,7 @@
         name="rear",
         out_shape=(shape((rows, model), low), shape((rows, model), low), shape((8, model), f32),
                    shape((shard, columns), low)),
-        in_specs=[vmem(), hbm(), vmem(), vmem()] + [hbm()] * 4 + [vmem()] * 3,
+        in_specs=[vmem(), hbm(), vmem(), vmem()] + [hbm()] * 7,
         out_specs=(hbm(), hbm(), vmem(), vmem()),
         scratch_shapes=[
             pltpu.VMEM((rows, model), low),
@@ -944,7 +945,7 @@
             pltpu.VMEM((rows, model), low),
             pltpu.VMEM((rows, model), f32),
             pltpu.VMEM((rows, model), f32),
-            pltpu.VMEM((rows, model), low),
+            pltpu.VMEM((4, rows, model), low),
             pltpu.VMEM((3, rows, model), low),
             pltpu.VMEM((2, rows // 2, model), low),
             pltpu.VMEM((2, rows, model), low),
@@ -958,19 +959,20 @@
             pltpu.SemaphoreType.DMA((copies,)),
         ],
         compiler_params=pltpu.CompilerParams(
-            vmem_limit_bytes=56 << 20, collective_id=2, has_side_effects=True),
+            vmem_limit_bytes=62 << 20, collective_id=2, has_side_effects=True),
         cost_estimate=pl.CostEstimate(flops=50_000_000_000, bytes_accessed=20 << 20, transcendentals=0),
     )(grad, normed, slab, gains, x, dh, hidden, *branch)
 
 
 def last_kernel(pieces_ref, qkv_ref, down_ref, gain_a_ref, gain_b_ref, out_qkv_ref, out_out_ref, out_gate_up_ref, out_down_ref,
-                gains_ref, block_ref, slots_ref, gain_own_ref, gain_take_ref, gain_slots_ref, local_sem, send_sem, recv_sem):
+                gains_ref, block_ref, slots_ref, out_own_ref, out_take_ref, out_part_ref, out_slots_ref, gain_own_ref, gain_take_ref, gain_slots_ref, local_sem, send_sem, recv_sem):
     low = jnp.bfloat16
     shard, columns = qkv_ref.shape
     model = gain_a_ref.shape[1]
     count = model // shard
     units = out_down_ref.shape[1] // 4
     width = columns // 3
+    part = model // 4
     mine, peers = seq_peers()
     place, sibling, _ = shard_peers(count)
     everyone = [lax.rem(place + k, count) for k in range(1, count)]
@@ -978,19 +980,26 @@
     ready = greet(peers, everyone)
     local = starter(local_sem)
     fills = [local(0, qkv_ref, block_ref.at[:, :columns]), local(1, down_ref, block_ref.at[:, columns:columns + units]),
-             local(2, pieces_ref, block_ref.at[:, columns + units:])]
+             local(2, pieces_ref.at[:, :2 * units], block_ref.at[:, columns + units:])]
+    out_fill = local(3, pieces_ref.at[:, 2 * units:], out_own_ref)
     gain_own_ref[0:1, :] = gain_a_ref[0:1, :]
     gain_own_ref[1:2, :] = gain_b_ref[0:1, :]
     gain_own_ref[2:8, :] = jnp.zeros((6, model), jnp.float32)
     for copy in fills:
         copy.wait()
     ready()
+    out_fill.wait()
+    base = 9 + len(everyone)
+    out_turn = [send(base + k, out_own_ref.at[:, span(peer, part)], out_take_ref.at[k], "seq", peer)
+                for k, peer in enumerate(peers)]
+    for k in (2, 0, 1):
+        out_turn[k].start()
     forward, arrivals, finish = spread(send, 0, block_ref, [slots_ref.at[k] for k in range(3)], peers)
     gain_sends = [send(6 + k, gain_own_ref, gain_take_ref.at[k], "fsdp", peer) for k, peer in enumerate(everyone)]
     for copy in gain_sends:
         copy.start()
 
-    def place_block(source, owner, first):
+    def place_block(source, owner):
         for b in range(3):
             out_qkv_ref[:, span(b * 4 + owner, width)] = source[:, b * width:(b + 1) * width]
         out_down_ref[:, span(owner, units)] = source[:, columns:columns + units]
@@ -1000,12 +1009,17 @@
                 out_gate_up_ref[:, pl.ds(pl.multiple_of((b * 4 + owner) * units + shift, TILE), size)] = (
                     source[:, at:at + size])
                 at += size
-        if first:
-            out_out_ref[...] = source[:, at:].astype(jnp.float32)
-        else:
-            out_out_ref[...] += source[:, at:].astype(jnp.float32)
-
-    place_block(block_ref, mine, True)
+
+    place_block(block_ref, mine)
+    value = out_own_ref[:, span(mine, part)].astype(jnp.float32)
+    for k in range(3):
+        out_turn[k].wait_recv()
+        value += out_take_ref[k].astype(jnp.float32)
+    out_part_ref[...] = value.astype(low)
+    out_out_ref[:, span(mine, part)] = out_part_ref[...]
+    out_sends = [send(base + 3 + k, out_part_ref, out_slots_ref.at[k], "seq", peer) for k, peer in enumerate(peers)]
+    for k in (2, 0, 1):
+        out_sends[k].start()
     forward()
     total = gain_own_ref[...]
     for k, copy in enumerate(gain_sends):
@@ -1017,11 +1031,13 @@
         copy.start()
     for k in range(3):
         arrivals[k]()
-        place_block(slots_ref.at[k], peers[k], False)
+        place_block(slots_ref.at[k], peers[k])
+        out_sends[k].wait_recv()
+        out_out_ref[:, span(peers[k], part)] = out_slots_ref[k]
     for copy in seq_sends:
         copy.wait()
     gains_ref[...] += gain_slots_ref[0] + gain_slots_ref[1] + gain_slots_ref[2]
-    for copy in gain_sends:
+    for copy in gain_sends + out_turn + out_sends:
         copy.wait_send()
     finish()
 
@@ -1033,14 +1049,14 @@
     count = model // shard
     f32 = jnp.float32
     shape = jax.ShapeDtypeStruct
-    wide = columns + units + pieces.shape[1]
-    copies = 9 + count
+    wide = columns + 3 * units
+    copies = 14 + count
     return pl.pallas_call(
         last_kernel,
         name="last",
         out_shape=(
             shape((shard, 4 * columns), low),
-            shape((shard, model), f32),
+            shape((shard, model), low),
             shape((shard, 8 * units), low),
             shape((shard, 4 * units), low),
             shape((8, model), f32),
@@ -1050,10 +1066,14 @@
         scratch_shapes=[
             pltpu.VMEM((shard, wide), low),
             pltpu.VMEM((3, shard, wide), low),
+            pltpu.VMEM((shard, model), low),
+            pltpu.VMEM((3, shard, model // 4), low),
+            pltpu.VMEM((shard, model // 4), low),
+            pltpu.VMEM((3, shard, model // 4), low),
             pltpu.VMEM((8, model), f32),
             pltpu.VMEM((count - 1, 8, model), f32),
             pltpu.VMEM((3, 8, model), f32),
-            pltpu.SemaphoreType.DMA((3,)),
+            pltpu.SemaphoreType.DMA((4,)),
             pltpu.SemaphoreType.DMA((copies,)),
             pltpu.SemaphoreType.DMA((copies,)),
         ],

time: 382 us -> 373 us (0.976)
  local copies, waits for them, and re-layouts: 13.5 us -> 8.25 us
  Pallas kernels: 338 us -> 333 us
    unnamed x38 -> x22, local copies, waits for them, and re-layouts: 10.2 us -> 3.87 us
    pallas_call x1, Pallas kernels: 48.6 us -> 43.5 us  [rear(): pl.pallas_call(rear_kernel, name='rear', out_shape=(shape((rows, model),...]
  transfers between devices with their start and end apart: 9 -> 9, of which waited for: 2 -> 2; matrix products, arithmetic and copies ran while one was open for 1% -> 1% of each run, Pallas kernels for 45% -> 46%
where the time goes in v1:
time: 373 us
  Pallas kernels  333 us (89%)
  between operations  14 us (4%)
  local copies, waits for them, and re-layouts  8.25 us (2%)
  waiting for transfers between devices  7.27 us (2%)
  starting transfers between devices  6.19 us (2%)
  other arithmetic  4.13 us (1%)
    pallas_call x1, Pallas kernels, middle(): pl.pallas_call(middle_kernel, name='middle', out_shape=(shape((rows, mode...  114 us
    pallas_call x1, Pallas kernels, attention_forward(): pl.pallas_call(forward_kernel, name='attention_forward', out_shape=(shape...  48.5 us
    pallas_call x1, Pallas kernels, last(): pl.pallas_call(last_kernel, name='last', out_shape=(shape((shard, 4 * col...  45.1 us
    pallas_call x1, Pallas kernels, rear(): pl.pallas_call(rear_kernel, name='rear', out_shape=(shape((rows, model),...  43.5 us
    pallas_call x1, Pallas kernels, gather_rows(): pl.pallas_call(gather_kernel, name='gather_rows', out_shape=jax.ShapeDtyp...  39 us
    pallas_call x1, Pallas kernels, attention_backward(): pl.pallas_call(backward_kernel, name='attention_backward', out_shape=jax....  38.7 us
  transfers between devices with their start and end apart: 9, of which 2 were waited for; matrix products, arithmetic and copies ran while one was open for 1% of the time, Pallas kernels for 46%

profile of v1, /device:TPU:0, one launch (start us, length us, event | category | flops | bytes accessed | tf_op | source)
XLA Modules:
  0.0 373.0 jit_solution(13541515754710081123)
XLA Ops:
  7.2 0.0 all-gather.3.cloned.1.call-start
  7.2 0.7 convert_bitcast_fusion
  7.9 0.1 copy.27
  8.1 1.1 dynamic-slice_convert_fusion.5
  9.1 0.7 fusion.1
  9.8 0.0 all-gather.3.cloned.1.call-update
  9.8 0.0 all-gather.5.cloned.1.call-start
  9.9 1.1 convert_element_type.27
  11.0 1.3 dynamic-slice_convert_fusion.2
  12.3 1.0 pad_maximum_fusion
  13.2 0.0 all-gather.5.cloned.1.call-update
  13.3 0.0 reduce-scatter.2.cloned.1.call-start
  13.3 0.0 copy-start.9
  13.3 0.0 copy-start.7
  13.3 0.0 copy-start.8
  13.4 39.0 %gather_rows.1.x_ref = bf16[2048,1024]{1,0:T(8,128)(2,1)} custom-call(bf16[512,1024]{1,0:T(8,128)(2,1)} %bitcast.25), custom_call_target="tpu_custom_call" | custom-call | flops 40000000000 | bytes 20971520 | tf_op jit(solution)/shard_map/gather_rows/pallas_call | solution.py:809
  52.4 1.5 collective-permute-start.2
  53.9 1.5 collective-permute-start.1
  55.4 0.6 collective-permute-start
  56.0 1.3 copy.28.perm_col_ref
  57.3 0.7 select_reduce_fusion
  58.0 48.5 %attention_forward.1 = (bf16[2048,768]{1,0:T(8,128)(2,1)}, bf16[2048,256]{1,0:T(8,128)(2,1)}, f32[256,2048]{1,0:T(8,128)}, f32[8,2048]{1,0:T(8,128)}, bf16[2048,1024]{1,0:T(8,128)(2,1)}, /*index=5*/f32[8,1024]{1,0:T(8,128)}) custom-call(s32[3]{0:T(128)} %bitcast.18, bf16[2048,1024]{1,0:T(8,128)(2,1)} %gather_rows.1.x_ref, ...), custom_call_target="tpu_custom_call" | custom-call | flops 24000000000 | bytes 16777216 | tf_op jit(solution)/shard_map/attention_forward/pallas_call | solution.py:231
  106.6 0.0 collective-permute-done.2.dy3_in
  106.6 0.0 collective-permute-done.1.dy2_in
  106.6 0.0 collective-permute-done.dy1_in
  106.6 4.2 %all-gather.5.cloned.1.call-done.weight_in = bf16[1024,3328]{1,0:T(8,128)(2,1)} async-done(((bf16[128,3328]{1,0:T(8,128)(2,1)}), bf16[1024,3328]{1,0:T(8,128)(2,1)}) %all-gather.5.cloned.1.call-update) | async-done | bytes 6815760 | tf_op jit(solution)/shard_map/all_gather | solution.py:1133
  110.8 114.1 %middle.1 = (f32[512,1024]{1,0:T(8,128)}, bf16[512,1024]{1,0:T(8,128)(2,1)}, bf16[512,1024]{1,0:T(8,128)(2,1)}, bf16[512,1024]{1,0:T(8,128)(2,1)}, bf16[512,1024...) custom-call(bf16[2048,256]{1,0:T(8,128)(2,1)} %get-tuple-element.42., ...), custom_call_target="tpu_custom_call" | custom-call | flops 60000002048 | bytes 41943040 | tf_op jit(solution)/shard_map/middle/pallas_call | solution.py:729
  224.9 0.0 copy-start.10
  224.9 0.0 reduce-scatter.2.cloned.1.call-update
  224.9 0.1 collective-permute-start.3
  225.0 0.1 collective-permute-start.4
  225.1 1.0 copy-done.10
  226.1 2.4 collective-permute-start.5
  228.5 38.7 %attention_backward.1.grad_ref = bf16[2048,768]{1,0:T(8,128)(2,1)} custom-call(s32[3]{0:T(128)} %bitcast.19, bf16[2048,256]{1,0:T(8,128)(2,1)} %get-tuple-element.46.grad_ref, bf16[2048,768]{1,0:T(8,128)(2,1)} %get-tuple-element.47.sorted_in, s32[1,2048]{1,0:T(1,128)} %perm_row_ref.3, s32[2048,1]{1,0:T(8,128)} %copy.28.perm_col_ref, s32[1,2048]{1,0:T(1,128)} %bitcast.17, ...), custom_call_target="tpu_custom_call" | custom-call | flops 40000000000 | bytes 16777216 | tf_op jit(solution)/shard_map/attention_backward/pallas_call | solution.py:263
  267.2 0.0 collective-permute-done.3.branch1_in
  267.2 3.0 collective-permute-done.4.branch2_in
  270.2 0.0 collective-permute-done.5.branch3_in
  270.2 43.5 %rear.1 = (bf16[512,1024]{1,0:T(8,128)(2,1)}, bf16[512,1024]{1,0:T(8,128)(2,1)}, f32[8,1024]{1,0:T(8,128)}, bf16[128,768]{1,0:T(8,128)(2,1)}) custom-call(bf16[2048,768]{1,0:T(8,128)(2,1)} %attention_backward.1.grad_ref, bf16[2048,1024]{1,0:T(8,128)(2,1)} %get-tuple-element.50.normed_in, bf16[1024,896]{1,0:T(8,128)(2,1)} %all-gather.3.cloned.1.call-done.slab_ref, ...), custom_call_target="tpu_custom_call" | custom-call | flops 49999998976 | bytes 20971520 | tf_op jit(solution)/shard_map/rear/pallas_call | solution.py:934
  313.8 0.0 reduce-scatter.2.cloned.1.call-done.pieces_ref
  313.8 0.0 copy-done.3
  313.8 0.0 copy-done.5
  313.8 0.0 copy-start.2
  313.8 1.1 copy-done.2
  315.0 0.9 copy-done.4
  315.9 0.8 copy-done.6
  316.6 45.1 %last.1 = (bf16[128,3072]{1,0:T(8,128)(2,1)S(1)}, bf16[128,1024]{1,0:T(8,128)(2,1)S(1)}, bf16[128,8192]{1,0:T(8,128)(2,1)S(1)}, bf16[128,4096]{1,0:T(8,128)(2,1)S(1)}, f32[8,1024]{1,0:T(8,128)S(1)}) custom-call(bf16[128,3072]{1,0:T(8,128)(2,1)S(1)} %copy-done.2, bf16[128,768]{1,0:T(8,128)(2,1)S(1)} %copy-done.4, bf16[128,1024]{1,0:T(8,128)(2,1)S(1)} %copy-done.3, ...), custom_call_target="tpu_custom_call" | custom-call | flops 40000000000 | bytes 20971520 | tf_op jit(solution)/shard_map/last/pallas_call | solution.py:1054
  361.8 0.5 slice_bitcast_fusion
  362.3 4.1 %widen.1 = (f32[128,3072]{1,0:T(8,128)}, f32[128,1024]{1,0:T(8,128)}, f32[128,8192]{1,0:T(8,128)}, f32[128,4096]{1,0:T(8,128)}, bf16[512,1024]{1,0:T(8,128)(2,1)}, /*index=5*/bf16[512,1024]{1,0:T(8,128)(2,1)}) custom-call(bf16[128,3072]{1,0:T(8,128)(2,1)S(1)} %get-tuple-element.61.refs_0_, bf16[128,1024]{1,0:T(8,128)(2,1)S(1)} %get-tuple-element.62.refs_1_, ...), custom_call_target="tpu_custom_call" | custom-call | tf_op jit(solution)/shard_map/widen/pallas_call | solution.py:1094
  (14 shorter events, 0.0 us)
Async XLA Ops:
  7.2 50.9 %all-gather.3.cloned.1.call-start = ((), (), s32[]{:S(2)}) async-start(), calls=%async_computation.1 | async-start | bytes 2064384 | tf_op jit(solution)/shard_map/all_gather | solution.py:1133
  9.8 100.9 %all-gather.5.cloned.1.call-start = ((), (), s32[]{:S(2)}) async-start(), calls=%async_computation.2 | async-start | bytes 7667712 | tf_op jit(solution)/shard_map/all_gather | solution.py:1133
  13.3 300.5 %reduce-scatter.2.cloned.1.call-start = ((), (), s32[]{:S(2)}) async-start(), calls=%async_computation.3 | async-start | bytes 7077888 | tf_op jit(solution)/shard_map/reduce_scatter | solution.py:1146
  13.3 39.1 %copy-start.9 = (bf16[1,512,1024]{2,1,0:T(8,128)(2,1)S(1)}, bf16[1,512,1024]{2,1,0:T(8,128)(2,1)}, u32[]{:S(2)}) copy-start(bf16[1,512,1024]{2,1,0:T(8,128)(2,1)} %param.18) | copy-start | bytes 3145732
  13.3 42.6 %copy-start.7 = (s32[1,2048]{1,0:T(1,128)S(1)}, s32[1,2048]{1,0:T(1,128)}, u32[]{:S(2)}) copy-start(s32[1,2048]{1,0:T(1,128)} %perm_row_ref.3) | copy-start | bytes 24580
  13.3 44.0 %copy-start.8 = (s32[1,3]{1,0:T(1,128)S(1)}, s32[1,3]{1,0:T(1,128)}, u32[]{:S(2)}) copy-start(s32[1,3]{1,0:T(1,128)} %param.20) | copy-start | bytes 40
  52.4 54.2 %collective-permute-start.2 = (bf16[512,1024]{1,0:T(8,128)(2,1)S(1)}, bf16[512,1024]{1,0:T(8,128)(2,1)}, u32[]{:S(2)}, u32[]{:S(2)}) collective-permute-start(bf16[512,1024]{1,0:T(8,128)(2,1)S(1)} %bitcast.22), channel_id=1, source_target_pairs={{0,24},{8,16},{16,8},{24,0},{1,25},{9,17},{17,9},{25,1},{2,26},{10... | collective-permute-start | bytes 3145736 | tf_op jit(solution)/shard_map/ppermute | solution.py:1107
  53.9 52.6 %collective-permute-start.1 = (bf16[512,1024]{1,0:T(8,128)(2,1)S(1)}, bf16[512,1024]{1,0:T(8,128)(2,1)}, u32[]{:S(2)}, u32[]{:S(2)}) collective-permute-start(bf16[512,1024]{1,0:T(8,128)(2,1)S(1)} %bitcast.23), channel_id=1, source_target_pairs={{0,16},{8,24},{16,0},{24,8},{1,17},{9,25},{17,1},{25,9},{2,18},{10... | collective-permute-start | bytes 3145736 | tf_op jit(solution)/shard_map/ppermute | solution.py:1107
  55.4 51.2 %collective-permute-start = (bf16[512,1024]{1,0:T(8,128)(2,1)S(1)}, bf16[512,1024]{1,0:T(8,128)(2,1)}, u32[]{:S(2)}, u32[]{:S(2)}) collective-permute-start(bf16[512,1024]{1,0:T(8,128)(2,1)S(1)} %bitcast.24), channel_id=1, source_target_pairs={{0,8},{8,0},{16,24},{24,16},{1,9},{9,1},{17,25},{25,17},{2,10},{10... | collective-permute-start | bytes 3145736 | tf_op jit(solution)/shard_map/ppermute | solution.py:1107
  224.9 1.2 copy-start.10
  224.9 42.2 %collective-permute-start.3 = (bf16[512,1024]{1,0:T(8,128)(2,1)}, bf16[512,1024]{1,0:T(8,128)(2,1)}, u32[]{:S(2)}, u32[]{:S(2)}) collective-permute-start(bf16[512,1024]{1,0:T(8,128)(2,1)} %get-tuple-element.54), channel_id=1, source_target_pairs={{0,8},{8,0},{16,24},{24,16},{1,9},{9,1},{17,25},{25,17},{2,10},{10... | collective-permute-start | bytes 3145736 | tf_op jit(solution)/shard_map/ppermute | solution.py:1107
  225.0 45.2 %collective-permute-start.4 = (bf16[512,1024]{1,0:T(8,128)(2,1)}, bf16[512,1024]{1,0:T(8,128)(2,1)}, u32[]{:S(2)}, u32[]{:S(2)}) collective-permute-start(bf16[512,1024]{1,0:T(8,128)(2,1)} %get-tuple-element.55), channel_id=1, source_target_pairs={{0,16},{8,24},{16,0},{24,8},{1,17},{9,25},{17,1},{25,9},{2,18},{10... | collective-permute-start | bytes 3145736 | tf_op jit(solution)/shard_map/ppermute | solution.py:1107
  226.1 44.1 %collective-permute-start.5 = (bf16[512,1024]{1,0:T(8,128)(2,1)S(1)}, bf16[512,1024]{1,0:T(8,128)(2,1)}, u32[]{:S(2)}, u32[]{:S(2)}) collective-permute-start(bf16[512,1024]{1,0:T(8,128)(2,1)S(1)} %copy-done.10), channel_id=1, source_target_pairs={{0,24},{8,16},{16,8},{24,0},{1,25},{9,17},{17,9},{25,1},{2,26},{10... | collective-permute-start | bytes 3145736 | tf_op jit(solution)/shard_map/ppermute | solution.py:1107
  270.2 43.6 %copy-start.3 = (bf16[128,1024]{1,0:T(8,128)(2,1)S(1)}, bf16[128,1024]{1,0:T(8,128)(2,1)}, u32[]{:S(2)}) copy-start(bf16[128,1024]{1,0:T(8,128)(2,1)} %get-tuple-element.58.down_ref) | copy-start | bytes 786436
  270.2 43.6 %copy-start.5 = (f32[8,1024]{1,0:T(8,128)S(1)}, f32[8,1024]{1,0:T(8,128)}, u32[]{:S(2)}) copy-start(f32[8,1024]{1,0:T(8,128)} %get-tuple-element.60.gain_b_ref) | copy-start | bytes 98308
  313.8 1.1 copy-start.2
  315.0 0.9 copy-start.4
  315.9 0.8 copy-start.6
  316.6 45.7 %copy-start = (bf16[512,1024]{1,0:T(8,128)(2,1)S(1)}, bf16[512,1024]{1,0:T(8,128)(2,1)}, u32[]{:S(2)}) copy-start(bf16[512,1024]{1,0:T(8,128)(2,1)} %get-tuple-element.65.refs_4_) | copy-start | bytes 3145732
  316.6 45.7 %copy-start.1 = (bf16[512,1024]{1,0:T(8,128)(2,1)S(1)}, bf16[512,1024]{1,0:T(8,128)(2,1)}, u32[]{:S(2)}) copy-start(bf16[512,1024]{1,0:T(8,128)(2,1)} %get-tuple-element.66.refs_5_) | copy-start | bytes 3145732
Sparse Core Ops, SparseCore 0:
  10.2 29.6 all-gather.2
  42.1 68.6 all-gather.4
  225.1 69.2 reduce-scatter.1

commit v2 on v1

--- a/solution.py
+++ b/solution.py
@@ -29,25 +29,25 @@
     group_len = src_ref.shape[0]
 
     def step(i, carry):
-        rows = pl.ds(pl.multiple_of(i * BLK, BLK), BLK)
-        pos = lax.broadcasted_iota(jnp.int32, (BLK, group_len), 0) + i * BLK
+        rows = pl.ds(pl.multiple_of(i * 1024, 1024), 1024)
+        pos = lax.broadcasted_iota(jnp.int32, (1024, group_len), 0) + i * 1024
         pick = (perm_row_ref[...] == pos).astype(jnp.float32).astype(jnp.bfloat16)
         dst_ref[rows, :] = dot(pick, src_ref[...]).astype(dst_ref.dtype)
         return carry
 
-    lax.fori_loop(0, group_len // BLK, step, 0)
+    lax.fori_loop(0, group_len // 1024, step, 0)
 
 
 def deal_rows(perm_col_ref, src_ref, dst_ref, out_ref, sems):
     group_len = src_ref.shape[0]
 
     def copy_out(i):
-        rows = pl.ds(pl.multiple_of(i * BLK, BLK), BLK)
+        rows = pl.ds(pl.multiple_of(i * 512, 512), 512)
         return pltpu.make_async_copy(dst_ref.at[rows, :], out_ref.at[rows, :], sems.at[i])
 
     def step(i, carry):
-        rows = pl.ds(pl.multiple_of(i * BLK, BLK), BLK)
-        pos = lax.broadcasted_iota(jnp.int32, (BLK, group_len), 1)
+        rows = pl.ds(pl.multiple_of(i * 512, 512), 512)
+        pos = lax.broadcasted_iota(jnp.int32, (512, group_len), 1)
         pick = (perm_col_ref[rows, :] == pos).astype(jnp.float32).astype(jnp.bfloat16)
         dst_ref[rows, :] = dot(pick, src_ref[...]).astype(dst_ref.dtype)
         copy_out(i).start()
@@ -57,8 +57,8 @@
         copy_out(i).wait()
         return carry
 
-    lax.fori_loop(0, group_len // BLK, step, 0)
-    lax.fori_loop(0, group_len // BLK, wait, 0)
+    lax.fori_loop(0, group_len // 512, step, 0)
+    lax.fori_loop(0, group_len // 512, wait, 0)
 
 
 def allowed_block(start_ref, cols, qb, kb):
@@ -83,15 +83,15 @@
     lax.fori_loop(0, model // 128, gain, 0)
 
     def project(i, carry):
-        rows = pl.ds(pl.multiple_of(i * BLK, BLK), BLK)
-        for r in range(0, BLK, 64):
-            part = pl.ds(pl.multiple_of(i * BLK + r, 64), 64)
+        rows = pl.ds(pl.multiple_of(i * 512, 512), 512)
+        for r in range(0, 512, 64):
+            part = pl.ds(pl.multiple_of(i * 512 + r, 64), 64)
             x = x_ref[part, :].astype(jnp.float32)
             normed_ref[part, :] = (x * rms_scale(x) * gains_ref[0:1, :]).astype(jnp.bfloat16)
         qkv_ref[rows, :] = dot(normed_ref[rows, :], slab_ref[:, :3 * width]).astype(jnp.bfloat16)
         return carry
 
-    lax.fori_loop(0, group_len // BLK, project, 0)
+    lax.fori_loop(0, group_len // 512, project, 0)
     outs = [pltpu.make_async_copy(normed_ref, normed_out, local_sem.at[0])]
     outs[0].start()
     sort_rows(perm_row_ref, qkv_ref, sorted_ref)
@@ -250,7 +250,7 @@
             pltpu.VMEM((width, group_len), jnp.bfloat16),
             pltpu.VMEM((group_len, width), jnp.bfloat16),
             pltpu.SemaphoreType.DMA((3,)),
-            pltpu.SemaphoreType.DMA((group_len // BLK,)),
+            pltpu.SemaphoreType.DMA((group_len // 512,)),
         ],
         compiler_params=pltpu.CompilerParams(vmem_limit_bytes=62 << 20),
         cost_estimate=pl.CostEstimate(flops=24_000_000_000, bytes_accessed=16 << 20, transcendentals=0),
@@ -277,7 +277,7 @@
             pltpu.VMEM((group_len, width), jnp.float32),
             pltpu.VMEM((group_len, columns), jnp.bfloat16),
             pltpu.SemaphoreType.DMA((2,)),
-            pltpu.SemaphoreType.DMA((group_len // BLK,)),
+            pltpu.SemaphoreType.DMA((group_len // 512,)),
         ],
         compiler_params=pltpu.CompilerParams(vmem_limit_bytes=62 << 20),
         cost_estimate=pl.CostEstimate(flops=40_000_000_000, bytes_accessed=16 << 20, transcendentals=0),
@@ -822,9 +822,9 @@
     )(x)
 
 
-def rear_kernel(grad_ref, normed_in, slab_ref, gains_ref, x_in, dh_in, hidden_in, branch0_in, branch1_in, branch2_in,
+def rear_kernel(grad_in, normed_in, slab_in, gains_ref, x_in, dh_in, hidden_in, branch0_in, branch1_in, branch2_in,
                 branch3_in, result_out, input_grad_out, gain_grad_ref, piece_ref,
-                result_ref, input_grad_ref, normed_ref, x_ref, dh_ref, hidden_ref, branch_ref, give_ref, transit_ref, take_ref, own_ref, term_ref,
+                grad_ref, slab_ref, result_ref, input_grad_ref, normed_ref, x_ref, dh_ref, hidden_ref, branch_ref, give_ref, transit_ref, take_ref, own_ref, term_ref,
                 twin_ref, total_ref, shard_take_ref, local_sem, send_sem, recv_sem):
     low = jnp.bfloat16
     rows, model = result_ref.shape
@@ -835,6 +835,8 @@
     place, sibling, others = shard_peers(count)
     send = sender(send_sem, recv_sem)
     local = starter(local_sem)
+    ready = greet(peers, [sibling] + others)
+    first_copies = [local(11, slab_in, slab_ref), local(12, grad_in, grad_ref)]
     normed_copy = local(0, normed_in, normed_ref)
     row_copies = [local(1, x_in, x_ref), local(2, dh_in, dh_ref)]
     result_copies = [local(3, hidden_in, hidden_ref)]
@@ -859,7 +861,8 @@
     def keep(cols, value):
         own_ref[:, cols] = value
 
-    ready = greet(peers, [sibling] + others)
+    for copy in first_copies:
+        copy.wait()
     hand(2, 0, half)
     ready()
     start_far, start_plain, merge, finish = collect(send, 0, give_ref, transit_ref, take_ref, peers, 2)
@@ -936,9 +939,11 @@
         name="rear",
         out_shape=(shape((rows, model), low), shape((rows, model), low), shape((8, model), f32),
                    shape((shard, columns), low)),
-        in_specs=[vmem(), hbm(), vmem(), vmem()] + [hbm()] * 7,
+        in_specs=[hbm(), hbm(), hbm(), vmem()] + [hbm()] * 7,
         out_specs=(hbm(), hbm(), vmem(), vmem()),
         scratch_shapes=[
+            pltpu.VMEM((group_len, columns), low),
+            pltpu.VMEM(slab.shape, low),
             pltpu.VMEM((rows, model), low),
             pltpu.VMEM((rows, model), low),
             pltpu.VMEM((group_len, model), low),
@@ -954,7 +959,7 @@
             pltpu.VMEM((count // 2, shard, columns), low),
             pltpu.VMEM((count // 2, shard, columns), low),
             pltpu.VMEM((count // 2, shard, columns), low),
-            pltpu.SemaphoreType.DMA((11,)),
+            pltpu.SemaphoreType.DMA((13,)),
             pltpu.SemaphoreType.DMA((copies,)),
             pltpu.SemaphoreType.DMA((copies,)),
         ],

time: 373 us -> 375 us (level)
  waiting for transfers between devices: 7.27 us -> 13 us
  Pallas kernels: 333 us -> 329 us
  transfers between devices with their start and end apart: 9 -> 9, of which waited for: 2 -> 2; matrix products, arithmetic and copies ran while one was open for 1% -> 1% of each run, Pallas kernels for 46% -> 45%
where the time goes in v2:
time: 375 us
  Pallas kernels  329 us (88%)
  between operations  14 us (4%)
  waiting for transfers between devices  13 us (3%)
  local copies, waits for them, and re-layouts  7.29 us (2%)
  starting transfers between devices  7.17 us (2%)
  other arithmetic  4.13 us (1%)
    pallas_call x1, Pallas kernels, middle(): pl.pallas_call(middle_kernel, name='middle', out_shape=(shape((rows, mode...  113 us
    pallas_call x1, Pallas kernels, attention_forward(): pl.pallas_call(forward_kernel, name='attention_forward', out_shape=(shape...  46.2 us
    pallas_call x1, Pallas kernels, last(): pl.pallas_call(last_kernel, name='last', out_shape=(shape((shard, 4 * col...  45.5 us
    pallas_call x1, Pallas kernels, rear(): pl.pallas_call(rear_kernel, name='rear', out_shape=(shape((rows, model),...  44.9 us
    pallas_call x1, Pallas kernels, gather_rows(): pl.pallas_call(gather_kernel, name='gather_rows', out_shape=jax.ShapeDtyp...  39 us
    pallas_call x1, Pallas kernels, attention_backward(): pl.pallas_call(backward_kernel, name='attention_backward', out_shape=jax....  37 us
  transfers between devices with their start and end apart: 9, of which 2 were waited for; matrix products, arithmetic and copies ran while one was open for 1% of the time, Pallas kernels for 45%

profile of v2, /device:TPU:0, one launch (start us, length us, event | category | flops | bytes accessed | tf_op | source)
XLA Modules:
  0.0 374.9 jit_solution(4721456384432174692)
XLA Ops:
  7.2 0.0 all-gather.3.cloned.1.call-start
  7.2 0.7 convert_bitcast_fusion
  7.9 0.1 copy.27
  8.1 1.1 dynamic-slice_convert_fusion.5
  9.1 0.7 fusion.1
  9.8 0.0 all-gather.3.cloned.1.call-update
  9.8 0.0 all-gather.5.cloned.1.call-start
  9.9 1.1 convert_element_type.27
  11.0 1.3 dynamic-slice_convert_fusion.2
  12.3 1.0 pad_maximum_fusion
  13.2 0.0 all-gather.5.cloned.1.call-update
  13.3 0.0 reduce-scatter.2.cloned.1.call-start
  13.3 0.0 copy-start.9
  13.3 0.0 copy-start.7
  13.3 0.0 copy-start.8
  13.4 39.0 %gather_rows.1.x_ref = bf16[2048,1024]{1,0:T(8,128)(2,1)} custom-call(bf16[512,1024]{1,0:T(8,128)(2,1)} %bitcast.25), custom_call_target="tpu_custom_call" | custom-call | flops 40000000000 | bytes 20971520 | tf_op jit(solution)/shard_map/gather_rows/pallas_call | solution.py:809
  52.4 0.0 copy-done.9
  52.4 1.5 collective-permute-start.2
  53.9 1.5 collective-permute-start.1
  55.4 0.6 collective-permute-start
  56.0 0.0 copy-done.7
  56.0 1.3 copy.28.perm_col_ref
  57.3 0.0 copy-done.8
  57.3 0.7 select_reduce_fusion
  58.0 46.2 %attention_forward.1 = (bf16[2048,768]{1,0:T(8,128)(2,1)}, bf16[2048,256]{1,0:T(8,128)(2,1)}, f32[256,2048]{1,0:T(8,128)}, f32[8,2048]{1,0:T(8,128)}, bf16[2048,1024]{1,0:T(8,128)(2,1)}, /*index=5*/f32[8,1024]{1,0:T(8,128)}) custom-call(s32[3]{0:T(128)} %bitcast.18, bf16[2048,1024]{1,0:T(8,128)(2,1)} %gather_rows.1.x_ref, ...), custom_call_target="tpu_custom_call" | custom-call | flops 24000000000 | bytes 16777216 | tf_op jit(solution)/shard_map/attention_forward/pallas_call | solution.py:231
  104.2 0.0 collective-permute-done.2.dy3_in
  104.2 0.0 collective-permute-done.1.dy2_in
  104.2 0.0 collective-permute-done.dy1_in
  104.3 6.5 %all-gather.5.cloned.1.call-done.weight_in = bf16[1024,3328]{1,0:T(8,128)(2,1)} async-done(((bf16[128,3328]{1,0:T(8,128)(2,1)}), bf16[1024,3328]{1,0:T(8,128)(2,1)}) %all-gather.5.cloned.1.call-update) | async-done | bytes 6815760 | tf_op jit(solution)/shard_map/all_gather | solution.py:1138
  110.8 112.7 %middle.1 = (f32[512,1024]{1,0:T(8,128)}, bf16[512,1024]{1,0:T(8,128)(2,1)}, bf16[512,1024]{1,0:T(8,128)(2,1)}, bf16[512,1024]{1,0:T(8,128)(2,1)}, bf16[512,1024...) custom-call(bf16[2048,256]{1,0:T(8,128)(2,1)} %get-tuple-element.42., ...), custom_call_target="tpu_custom_call" | custom-call | flops 60000002048 | bytes 41943040 | tf_op jit(solution)/shard_map/middle/pallas_call | solution.py:729
  223.4 0.0 copy-start.10
  223.4 0.0 reduce-scatter.2.cloned.1.call-update
  223.5 0.6 collective-permute-start.3
  224.0 0.6 collective-permute-start.4
  224.6 0.1 copy-done.10
  224.7 2.4 collective-permute-start.5
  227.0 37.0 %attention_backward.1.grad_in = bf16[2048,768]{1,0:T(8,128)(2,1)} custom-call(s32[3]{0:T(128)} %bitcast.19, bf16[2048,256]{1,0:T(8,128)(2,1)} %get-tuple-element.46.grad_ref, bf16[2048,768]{1,0:T(8,128)(2,1)} %get-tuple-element.47.sorted_in, s32[1,2048]{1,0:T(1,128)} %perm_row_ref.3, s32[2048,1]{1,0:T(8,128)} %copy.28.perm_col_ref, s32[1,2048]{1,0:T(1,128)} %bitcast.17, ...), custom_call_target="tpu_custom_call" | custom-call | flops 40000000000 | bytes 16777216 | tf_op jit(solution)/shard_map/attention_backward/pallas_call | solution.py:263
  264.0 0.0 collective-permute-done.3.branch1_in
  264.0 6.4 %collective-permute-done.4.branch2_in = bf16[512,1024]{1,0:T(8,128)(2,1)} collective-permute-done((bf16[512,1024]{1,0:T(8,128)(2,1)}, bf16[512,1024]{1,0:T(8,128)(2,1)}, u32[]{:S(2)}, u32[]{:S(2)}) %collective-permute-start.4) | collective-permute-done | bytes 1048608 | tf_op jit(solution)/shard_map/ppermute | solution.py:1112
  270.4 0.0 collective-permute-done.5.branch3_in
  270.4 44.9 %rear.1 = (bf16[512,1024]{1,0:T(8,128)(2,1)}, bf16[512,1024]{1,0:T(8,128)(2,1)}, f32[8,1024]{1,0:T(8,128)}, bf16[128,768]{1,0:T(8,128)(2,1)}) custom-call(bf16[2048,768]{1,0:T(8,128)(2,1)} %attention_backward.1.grad_in, bf16[2048,1024]{1,0:T(8,128)(2,1)} %get-tuple-element.50.normed_in, bf16[1024,896]{1,0:T(8,128)(2,1)} %all-gather.3.cloned.1.call-done.slab_ref.slab_in, ...), custom_call_target="tpu_custom_call" | custom-call | flops 49999998976 | bytes 20971520 | tf_op jit(solution)/shard_map/rear/pallas_call | solution.py:937
  315.3 0.0 reduce-scatter.2.cloned.1.call-done.pieces_ref
  315.4 1.1 copy-done.2
  316.5 0.9 copy-done.4
  317.4 0.8 copy-done.6
  318.2 45.5 %last.1 = (bf16[128,3072]{1,0:T(8,128)(2,1)S(1)}, bf16[128,1024]{1,0:T(8,128)(2,1)S(1)}, bf16[128,8192]{1,0:T(8,128)(2,1)S(1)}, bf16[128,4096]{1,0:T(8,128)(2,1)S(1)}, f32[8,1024]{1,0:T(8,128)S(1)}) custom-call(bf16[128,3072]{1,0:T(8,128)(2,1)S(1)} %copy-done.2, bf16[128,768]{1,0:T(8,128)(2,1)S(1)} %copy-done.4, bf16[128,1024]{1,0:T(8,128)(2,1)S(1)} %copy-done.3, ...), custom_call_target="tpu_custom_call" | custom-call | flops 40000000000 | bytes 20971520 | tf_op jit(solution)/shard_map/last/pallas_call | solution.py:1059
  363.7 0.5 slice_bitcast_fusion
  364.3 4.1 %widen.1 = (f32[128,3072]{1,0:T(8,128)}, f32[128,1024]{1,0:T(8,128)}, f32[128,8192]{1,0:T(8,128)}, f32[128,4096]{1,0:T(8,128)}, bf16[512,1024]{1,0:T(8,128)(2,1)}, /*index=5*/bf16[512,1024]{1,0:T(8,128)(2,1)}) custom-call(bf16[128,3072]{1,0:T(8,128)(2,1)S(1)} %get-tuple-element.61.refs_0_, bf16[128,1024]{1,0:T(8,128)(2,1)S(1)} %get-tuple-element.62.refs_1_, ...), custom_call_target="tpu_custom_call" | custom-call | tf_op jit(solution)/shard_map/widen/pallas_call | solution.py:1099
  (14 shorter events, 0.0 us)
Async XLA Ops:
  7.2 50.9 %all-gather.3.cloned.1.call-start = ((), (), s32[]{:S(2)}) async-start(), calls=%async_computation.1 | async-start | bytes 2064384 | tf_op jit(solution)/shard_map/all_gather | solution.py:1138
  9.8 100.9 %all-gather.5.cloned.1.call-start = ((), (), s32[]{:S(2)}) async-start(), calls=%async_computation.2 | async-start | bytes 7667712 | tf_op jit(solution)/shard_map/all_gather | solution.py:1138
  13.3 302.0 %reduce-scatter.2.cloned.1.call-start = ((), (), s32[]{:S(2)}) async-start(), calls=%async_computation.3 | async-start | bytes 7077888 | tf_op jit(solution)/shard_map/reduce_scatter | solution.py:1151
  13.3 39.1 %copy-start.9 = (bf16[1,512,1024]{2,1,0:T(8,128)(2,1)S(1)}, bf16[1,512,1024]{2,1,0:T(8,128)(2,1)}, u32[]{:S(2)}) copy-start(bf16[1,512,1024]{2,1,0:T(8,128)(2,1)} %param.18) | copy-start | bytes 3145732
  13.3 42.6 %copy-start.7 = (s32[1,2048]{1,0:T(1,128)S(1)}, s32[1,2048]{1,0:T(1,128)}, u32[]{:S(2)}) copy-start(s32[1,2048]{1,0:T(1,128)} %perm_row_ref.3) | copy-start | bytes 24580
  13.3 44.0 %copy-start.8 = (s32[1,3]{1,0:T(1,128)S(1)}, s32[1,3]{1,0:T(1,128)}, u32[]{:S(2)}) copy-start(s32[1,3]{1,0:T(1,128)} %param.20) | copy-start | bytes 40
  52.4 51.8 %collective-permute-start.2 = (bf16[512,1024]{1,0:T(8,128)(2,1)S(1)}, bf16[512,1024]{1,0:T(8,128)(2,1)}, u32[]{:S(2)}, u32[]{:S(2)}) collective-permute-start(bf16[512,1024]{1,0:T(8,128)(2,1)S(1)} %bitcast.22), channel_id=1, source_target_pairs={{0,24},{8,16},{16,8},{24,0},{1,25},{9,17},{17,9},{25,1},{2,26},{10... | collective-permute-start | bytes 3145736 | tf_op jit(solution)/shard_map/ppermute | solution.py:1112
  53.9 50.3 %collective-permute-start.1 = (bf16[512,1024]{1,0:T(8,128)(2,1)S(1)}, bf16[512,1024]{1,0:T(8,128)(2,1)}, u32[]{:S(2)}, u32[]{:S(2)}) collective-permute-start(bf16[512,1024]{1,0:T(8,128)(2,1)S(1)} %bitcast.23), channel_id=1, source_target_pairs={{0,16},{8,24},{16,0},{24,8},{1,17},{9,25},{17,1},{25,9},{2,18},{10... | collective-permute-start | bytes 3145736 | tf_op jit(solution)/shard_map/ppermute | solution.py:1112
  55.4 48.8 %collective-permute-start = (bf16[512,1024]{1,0:T(8,128)(2,1)S(1)}, bf16[512,1024]{1,0:T(8,128)(2,1)}, u32[]{:S(2)}, u32[]{:S(2)}) collective-permute-start(bf16[512,1024]{1,0:T(8,128)(2,1)S(1)} %bitcast.24), channel_id=1, source_target_pairs={{0,8},{8,0},{16,24},{24,16},{1,9},{9,1},{17,25},{25,17},{2,10},{10... | collective-permute-start | bytes 3145736 | tf_op jit(solution)/shard_map/ppermute | solution.py:1112
  223.4 1.2 copy-start.10
  223.5 40.5 %collective-permute-start.3 = (bf16[512,1024]{1,0:T(8,128)(2,1)}, bf16[512,1024]{1,0:T(8,128)(2,1)}, u32[]{:S(2)}, u32[]{:S(2)}) collective-permute-start(bf16[512,1024]{1,0:T(8,128)(2,1)} %get-tuple-element.54), channel_id=1, source_target_pairs={{0,8},{8,0},{16,24},{24,16},{1,9},{9,1},{17,25},{25,17},{2,10},{10... | collective-permute-start | bytes 3145736 | tf_op jit(solution)/shard_map/ppermute | solution.py:1112
  224.0 46.3 %collective-permute-start.4 = (bf16[512,1024]{1,0:T(8,128)(2,1)}, bf16[512,1024]{1,0:T(8,128)(2,1)}, u32[]{:S(2)}, u32[]{:S(2)}) collective-permute-start(bf16[512,1024]{1,0:T(8,128)(2,1)} %get-tuple-element.55), channel_id=1, source_target_pairs={{0,16},{8,24},{16,0},{24,8},{1,17},{9,25},{17,1},{25,9},{2,18},{10... | collective-permute-start | bytes 3145736 | tf_op jit(solution)/shard_map/ppermute | solution.py:1112
  224.7 45.7 %collective-permute-start.5 = (bf16[512,1024]{1,0:T(8,128)(2,1)S(1)}, bf16[512,1024]{1,0:T(8,128)(2,1)}, u32[]{:S(2)}, u32[]{:S(2)}) collective-permute-start(bf16[512,1024]{1,0:T(8,128)(2,1)S(1)} %copy-done.10), channel_id=1, source_target_pairs={{0,24},{8,16},{16,8},{24,0},{1,25},{9,17},{17,9},{25,1},{2,26},{10... | collective-permute-start | bytes 3145736 | tf_op jit(solution)/shard_map/ppermute | solution.py:1112
  270.4 44.9 %copy-start.3 = (bf16[128,1024]{1,0:T(8,128)(2,1)S(1)}, bf16[128,1024]{1,0:T(8,128)(2,1)}, u32[]{:S(2)}) copy-start(bf16[128,1024]{1,0:T(8,128)(2,1)} %get-tuple-element.58.down_ref) | copy-start | bytes 786436
  270.4 45.0 %copy-start.5 = (f32[8,1024]{1,0:T(8,128)S(1)}, f32[8,1024]{1,0:T(8,128)}, u32[]{:S(2)}) copy-start(f32[8,1024]{1,0:T(8,128)} %get-tuple-element.60.gain_b_ref) | copy-start | bytes 98308
  315.3 1.1 copy-start.2
  316.5 0.9 copy-start.4
  317.4 0.8 copy-start.6
  318.2 46.1 %copy-start = (bf16[512,1024]{1,0:T(8,128)(2,1)S(1)}, bf16[512,1024]{1,0:T(8,128)(2,1)}, u32[]{:S(2)}) copy-start(bf16[512,1024]{1,0:T(8,128)(2,1)} %get-tuple-element.65.refs_4_) | copy-start | bytes 3145732
  318.2 46.1 %copy-start.1 = (bf16[512,1024]{1,0:T(8,128)(2,1)S(1)}, bf16[512,1024]{1,0:T(8,128)(2,1)}, u32[]{:S(2)}) copy-start(bf16[512,1024]{1,0:T(8,128)(2,1)} %get-tuple-element.66.refs_5_) | copy-start | bytes 3145732
Sparse Core Ops, SparseCore 0:
  10.2 29.6 all-gather.2
  42.1 68.6 all-gather.4
  223.6 70.1 reduce-scatter.1

commit v3 on v2

--- a/solution.py
+++ b/solution.py
@@ -432,14 +432,14 @@
     return start_far, (plain[0].start, plain[1].start), merge, finish
 
 
-def middle_kernel(out_ref, x_ref, weight_in, gate_up_in, down_in, gains_ref, dy0_in, dy1_in, dy2_in, dy3_in,
+def middle_kernel(out_ref, x_in, weight_in, gate_up_in, down_in, gains_ref, dy0_in, dy1_in, dy2_in, dy3_in,
                   hidden_out, branch0_out, branch1_out, branch2_out, branch3_out, grads_out, dh_out,
                   do_ref, gain_grad_ref, down_piece_ref,
-                  raw_ref, tail_in, weight_ref, dy_ref, hidden_ref, branch_ref, grads_ref, mixed_ref, normed_ref, act_ref, dgu_ref,
+                  x_ref, raw_ref, tail_in, weight_ref, dy_ref, hidden_ref, branch_ref, grads_ref, mixed_ref, normed_ref, act_ref, dgu_ref,
                   give_ref, transit_ref, take_ref, own_ref, low_ref, do_give_ref, twin_ref, total_ref, shard_take_ref,
                   local_sem, send_sem, recv_sem):
     low = jnp.bfloat16
-    rows, model = x_ref.shape
+    rows, model = x_in.shape
     width = out_ref.shape[1]
     units = act_ref.shape[2]
     early = units - TILE
@@ -475,7 +475,7 @@
     for copy in raw:
         copy.wait()
     tail_in[...] = raw_ref[...].astype(low)
-    mixed_ref[:, span(mine, width)] = out_ref[span(mine, rows), :]
+    row_in = [local(17, out_ref.at[span(mine, rows), :], mixed_ref.at[:, span(mine, width)]), local(18, x_in, x_ref)]
     tail_ref = weight_ref.at[span(place, shard), tail_at:]
     tail_ref[...] = tail_in[...]
     ready()
@@ -517,7 +517,8 @@
         for k in range(3):
             turn[h][k].wait_recv()
         if h == 0:
-            out_in.wait()
+            for copy in [out_in] + row_in:
+                copy.wait()
 
         def project(c, h=h):
             cols = pl.ds(c, TILE)
@@ -738,9 +739,10 @@
             shape((8, model), f32),
             shape((shard, units), low),
         ),
-        in_specs=[vmem(), vmem(), hbm(), hbm(), hbm(), vmem()] + [hbm()] * 4,
+        in_specs=[hbm()] * 5 + [vmem()] + [hbm()] * 4,
         out_specs=(hbm(),) * 7 + (vmem(),) * 3,
         scratch_shapes=[
+            pltpu.VMEM((rows, model), low),
             pltpu.VMEM((shard, 3 * TILE), f32),
             pltpu.VMEM((shard, 3 * TILE), low),
             pltpu.VMEM((model, model + 3 * units), low),
@@ -761,7 +763,7 @@
             pltpu.VMEM((count // 2, shard, units), low),
             pltpu.VMEM((count // 2, shard, units), low),
             pltpu.VMEM((count // 2, shard, units), low),
-            pltpu.SemaphoreType.DMA((17,)),
+            pltpu.SemaphoreType.DMA((19,)),
             pltpu.SemaphoreType.DMA((copies,)),
             pltpu.SemaphoreType.DMA((copies,)),
         ],

time: 375 us -> 375 us (level)
  waiting for transfers between devices: 13 us -> 2.95 us
  Pallas kernels: 329 us -> 339 us
    pallas_call x1, Pallas kernels: 46.2 us -> 51.4 us  [attention_forward(): pl.pallas_call(forward_kernel, name='attention_forward', out_shape=(shape...]
    all_gather x2, waiting for transfers between devices: 6.51 us -> 1.28 us  [gather_weight(): lax.all_gather(jnp.concatenate(parts, axis=1), 'fsdp', axis=0, tiled=True)]
    ppermute x6, waiting for transfers between devices: 6.39 us -> 1.6 us  [swaps(): lax.ppermute(piece, 'seq', table)]
    pallas_call x1, Pallas kernels: 37 us -> 41.7 us  [attention_backward(): pl.pallas_call(backward_kernel, name='attention_backward', out_shape=jax....]
  transfers between devices with their start and end apart: 9 -> 9, of which waited for: 2 -> 2; matrix products, arithmetic and copies ran while one was open for 1% -> 1% of each run, Pallas kernels for 45% -> 47%
where the time goes in v3:
time: 375 us; the launch traced here: 374 us
  Pallas kernels  339 us (90%)
  between operations  14 us (4%)
  local copies, waits for them, and re-layouts  7.3 us (2%)
  starting transfers between devices  7.15 us (2%)
  other arithmetic  4.13 us (1%)
    pallas_call x1, Pallas kernels, middle(): pl.pallas_call(middle_kernel, name='middle', out_shape=(shape((rows, mode...  112 us
    pallas_call x1, Pallas kernels, attention_forward(): pl.pallas_call(forward_kernel, name='attention_forward', out_shape=(shape...  51.4 us
    pallas_call x1, Pallas kernels, last(): pl.pallas_call(last_kernel, name='last', out_shape=(shape((shard, 4 * col...  45.5 us
    pallas_call x1, Pallas kernels, rear(): pl.pallas_call(rear_kernel, name='rear', out_shape=(shape((rows, model),...  44.9 us
    pallas_call x1, Pallas kernels, attention_backward(): pl.pallas_call(backward_kernel, name='attention_backward', out_shape=jax....  41.7 us
    pallas_call x1, Pallas kernels, gather_rows(): pl.pallas_call(gather_kernel, name='gather_rows', out_shape=jax.ShapeDtyp...  39 us
  transfers between devices with their start and end apart: 9, of which 2 were waited for; matrix products, arithmetic and copies ran while one was open for 1% of the time, Pallas kernels for 47%

profile of v3, /device:TPU:0, one launch (start us, length us, event | category | flops | bytes accessed | tf_op | source)
XLA Modules:
  0.0 374.3 jit_solution(8187553847765697149)
XLA Ops:
  7.2 0.0 all-gather.3.cloned.1.call-start
  7.2 0.7 convert_bitcast_fusion
  7.9 0.1 copy.27
  8.1 1.1 dynamic-slice_convert_fusion.5
  9.1 0.7 fusion.1
  9.8 0.0 all-gather.3.cloned.1.call-update
  9.8 0.0 all-gather.5.cloned.1.call-start
  9.9 1.1 convert_element_type.27
  11.0 1.3 dynamic-slice_convert_fusion.2
  12.3 1.0 pad_maximum_fusion
  13.2 0.0 all-gather.5.cloned.1.call-update
  13.3 0.0 reduce-scatter.2.cloned.1.call-start
  13.3 0.0 copy-start.9
  13.3 0.0 copy-start.7
  13.3 0.0 copy-start.8
  13.4 39.0 %gather_rows.1.x_ref = bf16[2048,1024]{1,0:T(8,128)(2,1)} custom-call(bf16[512,1024]{1,0:T(8,128)(2,1)} %bitcast.25), custom_call_target="tpu_custom_call" | custom-call | flops 40000000000 | bytes 20971520 | tf_op jit(solution)/shard_map/gather_rows/pallas_call | solution.py:811
  52.4 0.0 copy-done.9
  52.4 1.5 collective-permute-start.2
  53.9 1.5 collective-permute-start.1
  55.4 0.6 collective-permute-start
  56.0 0.0 copy-done.7
  56.0 1.3 copy.28.perm_col_ref
  57.3 0.0 copy-done.8
  57.3 0.7 select_reduce_fusion
  58.0 51.4 %attention_forward.1 = (bf16[2048,768]{1,0:T(8,128)(2,1)}, bf16[2048,256]{1,0:T(8,128)(2,1)}, f32[256,2048]{1,0:T(8,128)}, f32[8,2048]{1,0:T(8,128)}, bf16[2048,1024]{1,0:T(8,128)(2,1)}, /*index=5*/f32[8,1024]{1,0:T(8,128)}) custom-call(s32[3]{0:T(128)} %bitcast.18, bf16[2048,1024]{1,0:T(8,128)(2,1)} %gather_rows.1.x_ref, ...), custom_call_target="tpu_custom_call" | custom-call | flops 24000000000 | bytes 16777216 | tf_op jit(solution)/shard_map/attention_forward/pallas_call | solution.py:231
  109.5 0.0 collective-permute-done.2.dy3_in
  109.5 0.0 collective-permute-done.1.dy2_in
  109.5 0.0 collective-permute-done.dy1_in
  109.5 1.3 all-gather.5.cloned.1.call-done.weight_in
  110.8 112.1 %middle.1 = (f32[512,1024]{1,0:T(8,128)}, bf16[512,1024]{1,0:T(8,128)(2,1)}, bf16[512,1024]{1,0:T(8,128)(2,1)}, bf16[512,1024]{1,0:T(8,128)(2,1)}, bf16[512,1024...) custom-call(bf16[2048,256]{1,0:T(8,128)(2,1)} %get-tuple-element.42., ...), custom_call_target="tpu_custom_call" | custom-call | flops 60000002048 | bytes 41943040 | tf_op jit(solution)/shard_map/middle/pallas_call | solution.py:730
  222.8 0.0 copy-start.10
  222.8 0.0 reduce-scatter.2.cloned.1.call-update
  222.9 0.6 collective-permute-start.3
  223.4 0.6 collective-permute-start.4
  224.0 0.1 copy-done.10
  224.1 2.4 collective-permute-start.5
  226.4 41.7 %attention_backward.1.grad_in = bf16[2048,768]{1,0:T(8,128)(2,1)} custom-call(s32[3]{0:T(128)} %bitcast.19, bf16[2048,256]{1,0:T(8,128)(2,1)} %get-tuple-element.46.grad_ref, bf16[2048,768]{1,0:T(8,128)(2,1)} %get-tuple-element.47.sorted_in, s32[1,2048]{1,0:T(1,128)} %perm_row_ref.3, s32[2048,1]{1,0:T(8,128)} %copy.28.perm_col_ref, s32[1,2048]{1,0:T(1,128)} %bitcast.17, ...), custom_call_target="tpu_custom_call" | custom-call | flops 40000000000 | bytes 16777216 | tf_op jit(solution)/shard_map/attention_backward/pallas_call | solution.py:263
  268.2 0.0 collective-permute-done.3.branch1_in
  268.2 1.6 collective-permute-done.4.branch2_in
  269.8 0.0 collective-permute-done.5.branch3_in
  269.8 44.9 %rear.1 = (bf16[512,1024]{1,0:T(8,128)(2,1)}, bf16[512,1024]{1,0:T(8,128)(2,1)}, f32[8,1024]{1,0:T(8,128)}, bf16[128,768]{1,0:T(8,128)(2,1)}) custom-call(bf16[2048,768]{1,0:T(8,128)(2,1)} %attention_backward.1.grad_in, bf16[2048,1024]{1,0:T(8,128)(2,1)} %get-tuple-element.50.normed_in, bf16[1024,896]{1,0:T(8,128)(2,1)} %all-gather.3.cloned.1.call-done.slab_ref.slab_in, ...), custom_call_target="tpu_custom_call" | custom-call | flops 49999998976 | bytes 20971520 | tf_op jit(solution)/shard_map/rear/pallas_call | solution.py:939
  314.7 0.0 reduce-scatter.2.cloned.1.call-done.pieces_ref
  314.8 1.1 copy-done.2
  315.9 0.9 copy-done.4
  316.8 0.8 copy-done.6
  317.6 45.5 %last.1 = (bf16[128,3072]{1,0:T(8,128)(2,1)S(1)}, bf16[128,1024]{1,0:T(8,128)(2,1)S(1)}, bf16[128,8192]{1,0:T(8,128)(2,1)S(1)}, bf16[128,4096]{1,0:T(8,128)(2,1)S(1)}, f32[8,1024]{1,0:T(8,128)S(1)}) custom-call(bf16[128,3072]{1,0:T(8,128)(2,1)S(1)} %copy-done.2, bf16[128,768]{1,0:T(8,128)(2,1)S(1)} %copy-done.4, bf16[128,1024]{1,0:T(8,128)(2,1)S(1)} %copy-done.3, ...), custom_call_target="tpu_custom_call" | custom-call | flops 40000000000 | bytes 20971520 | tf_op jit(solution)/shard_map/last/pallas_call | solution.py:1061
  363.1 0.5 slice_bitcast_fusion
  363.7 4.1 %widen.1 = (f32[128,3072]{1,0:T(8,128)}, f32[128,1024]{1,0:T(8,128)}, f32[128,8192]{1,0:T(8,128)}, f32[128,4096]{1,0:T(8,128)}, bf16[512,1024]{1,0:T(8,128)(2,1)}, /*index=5*/bf16[512,1024]{1,0:T(8,128)(2,1)}) custom-call(bf16[128,3072]{1,0:T(8,128)(2,1)S(1)} %get-tuple-element.61.refs_0_, bf16[128,1024]{1,0:T(8,128)(2,1)S(1)} %get-tuple-element.62.refs_1_, ...), custom_call_target="tpu_custom_call" | custom-call | tf_op jit(solution)/shard_map/widen/pallas_call | solution.py:1101
  (14 shorter events, 0.0 us)
Async XLA Ops:
  7.2 50.9 %all-gather.3.cloned.1.call-start = ((), (), s32[]{:S(2)}) async-start(), calls=%async_computation.1 | async-start | bytes 2064384 | tf_op jit(solution)/shard_map/all_gather | solution.py:1140
  9.8 100.9 %all-gather.5.cloned.1.call-start = ((), (), s32[]{:S(2)}) async-start(), calls=%async_computation.2 | async-start | bytes 7667712 | tf_op jit(solution)/shard_map/all_gather | solution.py:1140
  13.3 301.5 %reduce-scatter.2.cloned.1.call-start = ((), (), s32[]{:S(2)}) async-start(), calls=%async_computation.3 | async-start | bytes 7077888 | tf_op jit(solution)/shard_map/reduce_scatter | solution.py:1153
  13.3 39.1 %copy-start.9 = (bf16[1,512,1024]{2,1,0:T(8,128)(2,1)S(1)}, bf16[1,512,1024]{2,1,0:T(8,128)(2,1)}, u32[]{:S(2)}) copy-start(bf16[1,512,1024]{2,1,0:T(8,128)(2,1)} %param.18) | copy-start | bytes 3145732
  13.3 42.6 %copy-start.7 = (s32[1,2048]{1,0:T(1,128)S(1)}, s32[1,2048]{1,0:T(1,128)}, u32[]{:S(2)}) copy-start(s32[1,2048]{1,0:T(1,128)} %perm_row_ref.3) | copy-start | bytes 24580
  13.3 44.0 %copy-start.8 = (s32[1,3]{1,0:T(1,128)S(1)}, s32[1,3]{1,0:T(1,128)}, u32[]{:S(2)}) copy-start(s32[1,3]{1,0:T(1,128)} %param.20) | copy-start | bytes 40
  52.4 57.0 %collective-permute-start.2 = (bf16[512,1024]{1,0:T(8,128)(2,1)S(1)}, bf16[512,1024]{1,0:T(8,128)(2,1)}, u32[]{:S(2)}, u32[]{:S(2)}) collective-permute-start(bf16[512,1024]{1,0:T(8,128)(2,1)S(1)} %bitcast.22), channel_id=1, source_target_pairs={{0,24},{8,16},{16,8},{24,0},{1,25},{9,17},{17,9},{25,1},{2,26},{10... | collective-permute-start | bytes 3145736 | tf_op jit(solution)/shard_map/ppermute | solution.py:1114
  53.9 55.5 %collective-permute-start.1 = (bf16[512,1024]{1,0:T(8,128)(2,1)S(1)}, bf16[512,1024]{1,0:T(8,128)(2,1)}, u32[]{:S(2)}, u32[]{:S(2)}) collective-permute-start(bf16[512,1024]{1,0:T(8,128)(2,1)S(1)} %bitcast.23), channel_id=1, source_target_pairs={{0,16},{8,24},{16,0},{24,8},{1,17},{9,25},{17,1},{25,9},{2,18},{10... | collective-permute-start | bytes 3145736 | tf_op jit(solution)/shard_map/ppermute | solution.py:1114
  55.4 54.1 %collective-permute-start = (bf16[512,1024]{1,0:T(8,128)(2,1)S(1)}, bf16[512,1024]{1,0:T(8,128)(2,1)}, u32[]{:S(2)}, u32[]{:S(2)}) collective-permute-start(bf16[512,1024]{1,0:T(8,128)(2,1)S(1)} %bitcast.24), channel_id=1, source_target_pairs={{0,8},{8,0},{16,24},{24,16},{1,9},{9,1},{17,25},{25,17},{2,10},{10... | collective-permute-start | bytes 3145736 | tf_op jit(solution)/shard_map/ppermute | solution.py:1114
  222.8 1.2 copy-start.10
  222.9 45.3 %collective-permute-start.3 = (bf16[512,1024]{1,0:T(8,128)(2,1)}, bf16[512,1024]{1,0:T(8,128)(2,1)}, u32[]{:S(2)}, u32[]{:S(2)}) collective-permute-start(bf16[512,1024]{1,0:T(8,128)(2,1)} %get-tuple-element.54), channel_id=1, source_target_pairs={{0,8},{8,0},{16,24},{24,16},{1,9},{9,1},{17,25},{25,17},{2,10},{10... | collective-permute-start | bytes 3145736 | tf_op jit(solution)/shard_map/ppermute | solution.py:1114
  223.4 46.3 %collective-permute-start.4 = (bf16[512,1024]{1,0:T(8,128)(2,1)}, bf16[512,1024]{1,0:T(8,128)(2,1)}, u32[]{:S(2)}, u32[]{:S(2)}) collective-permute-start(bf16[512,1024]{1,0:T(8,128)(2,1)} %get-tuple-element.55), channel_id=1, source_target_pairs={{0,16},{8,24},{16,0},{24,8},{1,17},{9,25},{17,1},{25,9},{2,18},{10... | collective-permute-start | bytes 3145736 | tf_op jit(solution)/shard_map/ppermute | solution.py:1114
  224.1 45.7 %collective-permute-start.5 = (bf16[512,1024]{1,0:T(8,128)(2,1)S(1)}, bf16[512,1024]{1,0:T(8,128)(2,1)}, u32[]{:S(2)}, u32[]{:S(2)}) collective-permute-start(bf16[512,1024]{1,0:T(8,128)(2,1)S(1)} %copy-done.10), channel_id=1, source_target_pairs={{0,24},{8,16},{16,8},{24,0},{1,25},{9,17},{17,9},{25,1},{2,26},{10... | collective-permute-start | bytes 3145736 | tf_op jit(solution)/shard_map/ppermute | solution.py:1114
  269.8 45.0 %copy-start.3 = (bf16[128,1024]{1,0:T(8,128)(2,1)S(1)}, bf16[128,1024]{1,0:T(8,128)(2,1)}, u32[]{:S(2)}) copy-start(bf16[128,1024]{1,0:T(8,128)(2,1)} %get-tuple-element.58.down_ref) | copy-start | bytes 786436
  269.8 45.0 %copy-start.5 = (f32[8,1024]{1,0:T(8,128)S(1)}, f32[8,1024]{1,0:T(8,128)}, u32[]{:S(2)}) copy-start(f32[8,1024]{1,0:T(8,128)} %get-tuple-element.60.gain_b_ref) | copy-start | bytes 98308
  314.8 1.1 copy-start.2
  315.9 0.9 copy-start.4
  316.8 0.8 copy-start.6
  317.6 46.1 %copy-start = (bf16[512,1024]{1,0:T(8,128)(2,1)S(1)}, bf16[512,1024]{1,0:T(8,128)(2,1)}, u32[]{:S(2)}) copy-start(bf16[512,1024]{1,0:T(8,128)(2,1)} %get-tuple-element.65.refs_4_) | copy-start | bytes 3145732
  317.6 46.1 %copy-start.1 = (bf16[512,1024]{1,0:T(8,128)(2,1)S(1)}, bf16[512,1024]{1,0:T(8,128)(2,1)}, u32[]{:S(2)}) copy-start(bf16[512,1024]{1,0:T(8,128)(2,1)} %get-tuple-element.66.refs_5_) | copy-start | bytes 3145732
Sparse Core Ops, SparseCore 0:
  10.2 29.6 all-gather.2
  42.1 68.6 all-gather.4
  223.0 70.2 reduce-scatter.1
